TPU v7x, 128 devices: a whole 4x4x4 slice. The times are simulated.
128 devices in a mesh: grp: 8 (over x_hi, y), dom: 16 (over z, x_lo, core).
Axes of the slice: x: 4 (x_hi: 2, x_lo: 2; x = x_hi * 2 + x_lo), y: 4, z: 4, core: 2. Of those that a mesh axis runs over, the one named last changes fastest.
Arguments:
- features: bfloat16 [65536, 1024], P(('grp', 'dom')), may hold values from -6 to 6
- node_order: int32 [65536], P(('grp', 'dom')), may hold values from 0 to 65535, as said below
- block_cols: int32 [512, 16], P(('grp', 'dom')), may hold values from 0 to 63
- block_count: int32 [512], P(('grp', 'dom')), may hold values from 1 to 16, as said below
- block_vals: bfloat16 [512, 16, 128, 128], P(('grp', 'dom')), may hold values from -0.1875 to 0.1875
- weight: bfloat16 [1024, 512], replicated, may hold values from -0.1875 to 0.1875
- cotangent: bfloat16 [65536, 512], P(('grp', 'dom')), may hold values from -12 to 12
Outputs:
- hidden: bfloat16 [65536, 512], P(('grp', 'dom'))
- grad_weight: float32 [1024, 512], replicated
Inputs may be any that keep to these rules, and one draw needn't show every extreme that they name: `node_order`: A permutation of the crawl rows; the positions of one device's block of 512 take exactly 4 crawl rows from each device's block of 512 crawl rows. `block_count`: some row of blocks holds exactly 16 live blocks.
All inputs are finite; a program needn't handle non-finite values.
Results may differ from a plain program's by a relative error of at most 0.014.
Values may be sent and summed in bfloat16 or wider, within the bound.
A program may use at most 128 MiB of HBM per device.

v0:
```python
import jax
import jax.numpy as jnp
from jax import lax
from jax.sharding import PartitionSpec as P


def silu_slope(values):
    sig = jax.nn.sigmoid(values)
    return sig * (1.0 + values * (1.0 - sig))


def shards(features, node_order, block_cols, block_count, block_vals, weight, cotangent):
    row_count = features.shape[0]
    width_in = features.shape[1]
    hidden_units = weight.shape[1]
    tiles_dev = block_vals.shape[0]
    blocks = block_vals.shape[1]
    tile_size = block_vals.shape[-1]
    devices = lax.axis_size("grp") * lax.axis_size("dom")
    per_pair = row_count // devices
    source_device = node_order // row_count
    source_row = node_order % row_count
    ordering = jnp.argsort(source_device, stable=True)
    requests = source_row[ordering].reshape(devices, per_pair)
    asked_rows = lax.all_to_all(requests, ("grp", "dom"), split_axis=0, concat_axis=0, tiled=True)
    outgoing = features[asked_rows.reshape(-1)].reshape(devices, per_pair, width_in)
    arrived = lax.all_to_all(outgoing, ("grp", "dom"), split_axis=0, concat_axis=0, tiled=True)
    arrived = arrived.reshape(row_count, width_in)
    inverse = jnp.argsort(ordering)
    ordered = arrived[inverse]
    gathered = jnp.dot(
        lax.all_gather(ordered, "dom", axis=0, tiled=True),
        weight,
        preferred_element_type=jnp.float32,
    ).astype(jnp.bfloat16)
    panel_tiles = gathered.reshape(-1, tile_size, hidden_units)
    live_mask = lax.broadcasted_iota(jnp.int32, (tiles_dev, blocks), 1) < block_count[:, None]
    masked_vals = jnp.where(live_mask[:, :, None, None], block_vals, jnp.zeros((), jnp.bfloat16))
    selected = panel_tiles[block_cols]
    aggregate = jnp.einsum(
        "tkij,tkjh->tih", masked_vals, selected, preferred_element_type=jnp.float32
    )
    hidden = jax.nn.silu(aggregate).astype(jnp.bfloat16)
    cot_tiles = cotangent.reshape(tiles_dev, tile_size, hidden_units).astype(jnp.float32)
    grad_agg = (cot_tiles * silu_slope(aggregate)).astype(jnp.bfloat16)
    contrib = jnp.einsum(
        "tkij,tih->tkjh", masked_vals, grad_agg, preferred_element_type=jnp.float32
    )
    partial_value = jnp.zeros((panel_tiles.shape[0], tile_size, hidden_units), jnp.float32)
    partial_value = partial_value.at[block_cols.reshape(-1)].add(
        contrib.reshape(-1, tile_size, hidden_units)
    )
    partial_value = partial_value.reshape(-1, hidden_units).astype(jnp.bfloat16)
    grad_rows = lax.psum_scatter(
        partial_value.astype(jnp.float32).astype(jnp.bfloat16),
        "dom",
        scatter_dimension=0,
        tiled=True,
    ).astype(jnp.float32)
    local_grad = jnp.dot(ordered.astype(jnp.float32).T, grad_rows, precision=lax.Precision.HIGHEST)
    grad_weight = lax.psum(local_grad, ("grp", "dom"))
    return (hidden.reshape(row_count, hidden_units), grad_weight)


def solution(mesh):
    placed = (
        P(("grp", "dom"), None),
        P(("grp", "dom")),
        P(("grp", "dom"), None),
        P(("grp", "dom")),
        P(("grp", "dom"), None, None, None),
        P(),
        P(("grp", "dom"), None),
    )
    return jax.shard_map(
        shards,
        mesh=mesh,
        in_specs=placed,
        out_specs=(P(("grp", "dom"), None), P()),
        check_vma=False,
    )
```

profile of v0, /device:TPU:1, one launch (start us, length us, event | category | flops | bytes accessed | tf_op | source)
XLA Modules:
  0.0 514.7 jit_solution(14806534300630540247)
XLA Ops:
  7.2 0.8 add_select_fusion
  8.0 3.8 sort.34
  11.7 3.5 gather_fusion
  15.4 20.9 %all_to_all.14 = s32[128,1,4]{2,1,0:T(1,128)S(1)} all-to-all(s32[128,1,4]{2,1,0:T(1,128)S(1)} %bitcast.29), channel_id=1, replica_groups=mesh['grp'=8,'dom'=16] {'grp','dom'}, dimensions={0} | all-to-all | bytes 4096 | tf_op jit(solution)/shard_map/all_to_all | solution.py:25
  36.2 0.5 broadcast.90
  36.7 0.8 reduce.3
  37.7 4.1 gather_fusion.1
  41.8 1.2 reshape.111
  43.0 4.4 all-to-all-start.1
  47.5 3.8 sort.35
  51.3 15.2 %all-to-all-done.1 = bf16[128,4,1024]{2,1,0:T(4,128)(2,1)S(1)} async-done(((bf16[128,4,1024]{2,1,0:T(4,128)(2,1)}), bf16[128,4,1024]{2,1,0:T(4,128)(2,1)S(1)}, u32[]{:S(2)}, u32[]{:S(2)}) %all-to-all-start.1) | async-done | bytes 1048608 | tf_op jit(solution)/shard_map/all_to_all | solution.py:27
  66.8 2.8 gather_fusion.2
  70.1 88.1 %all-gather.3.cloned.1.call-done = bf16[8192,1024]{1,0:T(8,128)(2,1)} async-done(((bf16[512,1024]{1,0:T(8,128)(2,1)}), bf16[8192,1024]{1,0:T(8,128)(2,1)}) %all-gather.3.cloned.1.call-update) | async-done | bytes 16777232 | tf_op jit(solution)/shard_map/all_gather | solution.py:32
  158.2 16.9 %convolution_convert_fusion = bf16[8192,512]{1,0:T(8,128)(2,1)} fusion(bf16[8192,1024]{1,0:T(8,128)(2,1)} %all-gather.3.cloned.1.call-done, bf16[1024,512]{1,0:T(8,128)(2,1)S(1)} %copy-done), kind=kOutput, calls=%fused_computation.5 | convolution fusion | flops 8594128896 | bytes 26214400 | tf_op jit(solution)/shard_map/dot_general | solution.py:31
  175.1 9.1 %gather_fusion.3 = bf16[64,128,512]{2,1,0:T(8,128)(2,1)} fusion(bf16[64,128,512]{2,1,0:T(8,128)(2,1)} %bitcast.27, s32[1024]{0:T(1024)S(1)} %pad_clamp_fusion), kind=kCustom, calls=%fused_computation.3 | custom fusion | bytes 16777472 | tf_op jit(solution)/shard_map/gather | solution.py:39
  184.1 5.7 %multiply_convert_fusion = (bf16[4,128,512]{2,1,0:T(8,128)(2,1)}, f32[4,128,512]{2,1,0:T(8,128)S(1)}) fusion(bf16[4,16,128,512]{3,2,1,0:T(8,128)(2,1)} %bitcast.26, bf16[4,16,128,128]{3,2,1,0:T(8,128)(2,1)S(1)} %copy-done.3, pred[4,16]{1,0:T(4,128)(4,1)S(1)} %iota_compare_fusion), kind=kOutput, calls=%fused_computation.12 | convolution fusion | flops 1076101120 | bytes 12058688 | tf_op jit(solution)/shard_map/tkij,tkjh->tih/dot_general | solution.py:40
  189.8 8.2 %fusion = f32[4,16,128,512]{3,2,1,0:T(8,128)} fusion(bf16[4,16,128,128]{3,2,1,0:T(8,128)(2,1)S(1)} %copy-done.3, pred[4,16]{1,0:T(4,128)(4,1)S(1)} %iota_compare_fusion, bf16[4,128,512]{2,1,0:T(8,128)(2,1)S(1)} %bitcast.28, f32[4,128,512]{2,1,0:T(8,128)S(1)} %get-tuple-element.9), kind=kOutput, calls=%fused_computation.7 | convolution fusion | flops 1077411840 | bytes 20447296 | tf_op jit(solution)/shard_map/tkij,tih->tkjh/dot_general | solution.py:46
  198.1 7.9 %broadcast_in_dim.33 = f32[64,128,512]{2,1,0:T(8,128)} broadcast(f32[]{:T(128)} %constant.42.clone.1), dimensions={} | broadcast | bytes 16777220 | tf_op jit(solution)/shard_map/broadcast_in_dim | solution.py:49
  205.9 37.0 %scatter_fusion = f32[64,128,512]{2,1,0:T(8,128)} fusion(f32[64,128,512]{2,1,0:T(8,128)} %broadcast_in_dim.33, s32[64]{0:T(128)S(1)} %fusion.9, f32[64,128,512]{2,1,0:T(8,128)} %bitcast.24), kind=kCustom, calls=%fused_computation.4 | custom fusion | flops 4194304 | bytes 50331904 | tf_op jit(solution)/shard_map/scatter-add | solution.py:50
  242.9 9.0 %convert_element_type.30 = bf16[64,128,512]{2,1,0:T(8,128)(2,1)} convert(f32[64,128,512]{2,1,0:T(8,128)} %scatter_fusion) | non-fusion elementwise | flops 4194304 | bytes 25165824 | tf_op jit(solution)/shard_map/convert_element_type | solution.py:53
  252.0 96.8 %reduce-scatter.2.cloned.1.call-done = bf16[512,512]{1,0:T(8,128)(2,1)} async-done(((bf16[8192,512]{1,0:T(8,128)(2,1)}), bf16[512,512]{1,0:T(8,128)(2,1)}) %reduce-scatter.2.cloned.1.call-update) | async-done | bytes 524304 | tf_op jit(solution)/shard_map/reduce_scatter | solution.py:54
  348.8 3.1 fusion.13
  351.9 153.2 %all-reduce.2.cloned.1.call-done = f32[1024,512]{1,0:T(8,128)} async-done(((f32[1024,512]{1,0:T(8,128)}), f32[1024,512]{1,0:T(8,128)}) %all-reduce.2.cloned.1.call-update) | async-done | bytes 2097168 | tf_op jit(solution)/shard_map/psum | solution.py:61
  505.1 3.1 copy.18
  (37 shorter events, 1.2 us)
Async XLA Ops:
  7.2 151.0 %copy-start = (bf16[1024,512]{1,0:T(8,128)(2,1)S(1)}, bf16[1024,512]{1,0:T(8,128)(2,1)}, u32[]{:S(2)}) copy-start(bf16[1024,512]{1,0:T(8,128)(2,1)} %param.12) | copy-start | bytes 3145732
  41.8 28.0 %copy-start.5 = (s32[4,16]{1,0:T(4,128)S(1)}, s32[4,16]{1,0:T(4,128)}, u32[]{:S(2)}) copy-start(s32[4,16]{1,0:T(4,128)} %param.9) | copy-start | bytes 772
  41.8 28.2 %copy-start.6 = (s32[4]{0:T(128)S(1)}, s32[4]{0:T(128)}, u32[]{:S(2)}) copy-start(s32[4]{0:T(128)} %param.10) | copy-start | bytes 52
  43.0 23.5 %all-to-all-start.1 = ((bf16[128,4,1024]{2,1,0:T(4,128)(2,1)}), bf16[128,4,1024]{2,1,0:T(4,128)(2,1)S(1)}, u32[]{:S(2)}, u32[]{:S(2)}) async-start(bf16[128,4,1024]{2,1,0:T(4,128)(2,1)} %reshape.111), calls=%async_computation.1 | async-start | bytes 2097152 | tf_op jit(solution)/shard_map/all_to_all | solution.py:27
  47.4 110.7 %all-gather.3.cloned.1.call-start = ((), (), s32[]{:S(2)}) async-start(), calls=%async_computation.5 | async-start | bytes 17825792 | tf_op jit(solution)/shard_map/all_gather | solution.py:32
  69.6 279.2 %reduce-scatter.2.cloned.1.call-start = ((), (), s32[]{:S(2)}) async-start(), calls=%async_computation.3 | async-start | bytes 8912896 | tf_op jit(solution)/shard_map/reduce_scatter | solution.py:54
  175.1 9.1 %copy-start.3 = (bf16[4,16,128,128]{3,2,1,0:T(8,128)(2,1)S(1)}, bf16[4,16,128,128]{3,2,1,0:T(8,128)(2,1)}, u32[]{:S(2)}) copy-start(bf16[4,16,128,128]{3,2,1,0:T(8,128)(2,1)} %param.11) | copy-start | bytes 6291460
  184.1 5.7 %copy-start.4 = (bf16[512,512]{1,0:T(8,128)(2,1)S(1)}, bf16[512,512]{1,0:T(8,128)(2,1)}, u32[]{:S(2)}) copy-start(bf16[512,512]{1,0:T(8,128)(2,1)} %param.13) | copy-start | bytes 1572868
  251.9 96.9 %copy-start.2 = (bf16[512,1024]{1,0:T(8,128)(2,1)S(1)}, bf16[512,1024]{1,0:T(8,128)(2,1)}, u32[]{:S(2)}) copy-start(bf16[512,1024]{1,0:T(8,128)(2,1)} %gather_fusion.2) | copy-start | bytes 3145732
  251.9 256.2 %copy-start.1 = (bf16[1024,512]{1,0:T(8,128)(2,1)S(1)}, bf16[1024,512]{1,0:T(8,128)(2,1)}, u32[]{:S(2)}) copy-start(bf16[1024,512]{1,0:T(8,128)(2,1)} %param.12) | copy-start | bytes 3145732
  251.9 253.1 %all-reduce.2.cloned.1.call-start = ((), (), s32[]{:S(2)}) async-start(), calls=%async_computation.4 | async-start | bytes 4194304 | tf_op jit(solution)/shard_map/psum | solution.py:61
Sparse Core Ops, SparseCore 0:
  69.7 88.4 all-gather.2
  252.1 96.6 reduce-scatter.1
  354.2 150.8 all-reduce.1
where the time goes:
time: 515 us
  waiting for transfers between devices  353 us (69%)
  other arithmetic  55.2 us (11%)
  matrix products  33.9 us (7%)
  local copies, waits for them, and re-layouts  32.8 us (6%)
  blocking collectives  20.9 us (4%)
  between operations  13.9 us (3%)
    psum x1, waiting for transfers between devices, shards(): grad_weight = lax.psum(local_grad, ('grp', 'dom'))  153 us
    reduce_scatter x1, waiting for transfers between devices, shards(): lax.psum_scatter(partial_value.astype(jnp.float32).astype(jnp.bfloat16),...  96.8 us
    all_gather x1, waiting for transfers between devices, shards(): lax.all_gather(ordered, 'dom', axis=0, tiled=True)  88.1 us
    scatter-add x1, other arithmetic, shards(): partial_value.at[block_cols.reshape(-1)]  37 us
    all_to_all x1, blocking collectives, shards(): lax.all_to_all(requests, ('grp', 'dom'), split_axis=0, concat_axis=0, til...  20.9 us
    dot_general x1, matrix products, shards(): jnp.dot(lax.all_gather(ordered, 'dom', axis=0, tiled=True), weight, prefe...  16.9 us
    all_to_all x1, waiting for transfers between devices, shards(): lax.all_to_all(outgoing, ('grp', 'dom'), split_axis=0, concat_axis=0, til...  15.2 us
  transfers between devices with their start and end apart: 4, of which 4 were waited for; matrix products, arithmetic and copies ran while one was open for 1% of the time, Pallas kernels for 0%

commit v1 on v0

v1 whole, which is shorter than its diff:
```python
import jax
import jax.numpy as jnp
from jax import lax
from jax.sharding import PartitionSpec as P


def silu_slope(values):
    sig = jax.nn.sigmoid(values)
    return sig * (1.0 + values * (1.0 - sig))


def regroup(features, node_order):
    row_count, width_in = features.shape
    devices = lax.axis_size("grp") * lax.axis_size("dom")
    per_pair = row_count // devices
    source_device = node_order // row_count
    source_row = node_order % row_count
    ordering = jnp.argsort(source_device, stable=True)
    requests = source_row[ordering].reshape(devices, per_pair)
    asked_rows = lax.all_to_all(requests, ("grp", "dom"), split_axis=0, concat_axis=0, tiled=True)
    outgoing = features[asked_rows.reshape(-1)].reshape(devices, per_pair, width_in)
    arrived = lax.all_to_all(outgoing, ("grp", "dom"), split_axis=0, concat_axis=0, tiled=True)
    arrived = arrived.reshape(row_count, width_in)
    inverse = jnp.argsort(ordering)
    return arrived[inverse]


def shards(features, node_order, block_cols, block_count, block_vals, weight, cotangent):
    row_count, width_in = features.shape
    hidden_units = weight.shape[1]
    tiles_dev, blocks, tile_size, _ = block_vals.shape
    ordered = regroup(features, node_order)
    everyone = lax.all_gather(ordered, "dom", axis=0, tiled=True)
    panel_tiles = everyone.reshape(-1, tile_size, width_in)
    live_mask = lax.broadcasted_iota(jnp.int32, (tiles_dev, blocks), 1) < block_count[:, None]
    masked_vals = jnp.where(live_mask[:, :, None, None], block_vals, jnp.zeros((), jnp.bfloat16))
    selected = panel_tiles[block_cols]
    mixed = jnp.einsum("tkij,tkjf->tif", masked_vals, selected, preferred_element_type=jnp.float32)
    mixed = mixed.astype(jnp.bfloat16).reshape(row_count, width_in)
    aggregate = jnp.dot(mixed, weight, preferred_element_type=jnp.float32)
    hidden = jax.nn.silu(aggregate).astype(jnp.bfloat16)
    grad_agg = (cotangent.astype(jnp.float32) * silu_slope(aggregate)).astype(jnp.bfloat16)
    local_grad = lax.dot_general(
        mixed, grad_agg, (((0,), (0,)), ((), ())), preferred_element_type=jnp.float32
    )
    grad_weight = lax.psum(local_grad, ("grp", "dom"))
    return (hidden, grad_weight)


def solution(mesh):
    placed = (
        P(("grp", "dom"), None),
        P(("grp", "dom")),
        P(("grp", "dom"), None),
        P(("grp", "dom")),
        P(("grp", "dom"), None, None, None),
        P(),
        P(("grp", "dom"), None),
    )
    return jax.shard_map(
        shards,
        mesh=mesh,
        in_specs=placed,
        out_specs=(P(("grp", "dom"), None), P()),
        check_vma=False,
    )
```

time: 515 us -> 342 us (0.66)
  waiting for transfers between devices: 353 us -> 255 us
  other arithmetic: 55.2 us -> 9.24 us
  matrix products: 33.9 us -> 11.2 us
  local copies, waits for them, and re-layouts: 32.8 us -> 27.2 us
    reduce_scatter x1 -> x0, waiting for transfers between devices: 96.8 us -> none  [shards(): lax.psum_scatter(partial_value.astype(jnp.float32).astype(jnp.bfloat16),...]
    scatter-add x1 -> x0, other arithmetic: 37 us -> none  [shards(): partial_value.at[block_cols.reshape(-1)]]
    dot_general x4 -> x3, matrix products: 33.9 us -> 11.2 us  [the longest x1 7.32 us: shards(): jnp.einsum('tkij,tkjf->tif', masked_vals, selected, preferred_element_typ...]
    convert_element_type x1 -> x0, other arithmetic: 9.03 us -> none  [shards(): partial_value = partial_value.reshape(-1, hidden_units).astype(jnp.bfloat16)]
    broadcast_in_dim x1 -> x0, local copies, waits for them, and re-layouts: 7.87 us -> none  [shards(): jnp.zeros((panel_tiles.shape[0], tile_size, hidden_units), jnp.float32)]
  transfers between devices with their start and end apart: 4 -> 3, of which waited for: 4 -> 3; matrix products, arithmetic and copies ran while one was open for 1% -> 1% of each run, Pallas kernels for 0% -> 0%
where the time goes in v1:
time: 342 us
  waiting for transfers between devices  255 us (75%)
  local copies, waits for them, and re-layouts  27.2 us (8%)
  blocking collectives  20.9 us (6%)
  between operations  14.2 us (4%)
  matrix products  11.2 us (3%)
  other arithmetic  9.24 us (3%)
  starting transfers between devices  4.48 us (1%)
    psum x1, waiting for transfers between devices, shards(): grad_weight = lax.psum(local_grad, ('grp', 'dom'))  151 us
    all_gather x1, waiting for transfers between devices, shards(): everyone = lax.all_gather(ordered, 'dom', axis=0, tiled=True)  88.4 us
    all_to_all x1, blocking collectives, regroup(): lax.all_to_all(requests, ('grp', 'dom'), split_axis=0, concat_axis=0, til...  20.9 us
    all_to_all x1, waiting for transfers between devices, regroup(): lax.all_to_all(outgoing, ('grp', 'dom'), split_axis=0, concat_axis=0, til...  15.2 us
    gather x1, local copies, waits for them, and re-layouts, shards(): selected = panel_tiles[block_cols]  13.5 us
    dot_general x1, matrix products, shards(): jnp.einsum('tkij,tkjf->tif', masked_vals, selected, preferred_element_typ...  7.32 us
  transfers between devices with their start and end apart: 3, of which 3 were waited for; matrix products, arithmetic and copies ran while one was open for 1% of the time, Pallas kernels for 0%

profile of v1, /device:TPU:1, one launch (start us, length us, event | category | flops | bytes accessed | tf_op | source)
XLA Modules:
  0.0 341.9 jit_solution(17413993428679002675)
XLA Ops:
  7.2 0.8 add_select_fusion
  8.0 3.8 %sort.34 = (s32[512]{0:T(512)}, s32[512]{0:T(512)S(1)}) sort(s32[512]{0:T(512)S(1)} %get-tuple-element.6, s32[512]{0:T(512)S(1)} %iota.16), dimensions={0}, to_apply=%region_0.1 | sort | flops 4608 | bytes 8192 | tf_op jit(solution)/shard_map/jit(argsort)/sort | solution.py:18
  11.7 3.5 %gather_fusion = s32[512]{0:T(512)S(1)} fusion(s32[512]{0:T(512)S(1)} %get-tuple-element.7, s32[1024]{0:T(1024)S(1)} %pad_clamp_fusion.3), kind=kCustom, calls=%fused_computation | custom fusion | bytes 6144 | tf_op jit(solution)/shard_map/gather | solution.py:19
  15.2 0.1 all_to_all.9
  15.4 20.9 %all_to_all.14 = s32[128,1,4]{2,1,0:T(1,128)S(1)} all-to-all(s32[128,1,4]{2,1,0:T(1,128)S(1)} %bitcast.16), channel_id=1, replica_groups=mesh['grp'=8,'dom'=16] {'grp','dom'}, dimensions={0} | all-to-all | bytes 4096 | tf_op jit(solution)/shard_map/all_to_all | solution.py:20
  36.2 0.5 broadcast.76
  36.7 0.8 reduce.3
  37.6 0.1 reshape.71
  37.7 2.1 gather_fusion.1
  39.8 1.2 reshape.72
  41.0 4.4 %all-to-all-start.1 = ((bf16[128,4,1024]{2,1,0:T(4,128)(2,1)}), bf16[128,4,1024]{2,1,0:T(4,128)(2,1)S(1)}, u32[]{:S(2)}, u32[]{:S(2)}) async-start(bf16[128,4,1024]{2,1,0:T(4,128)(2,1)} %reshape.72), calls=%async_computation.1 | async-start | bytes 2097152 | tf_op jit(solution)/shard_map/all_to_all | solution.py:22
  45.4 3.8 %sort.35 = (s32[512]{0:T(512)}, s32[512]{0:T(512)S(1)}) sort(s32[512]{0:T(512)S(1)} %get-tuple-element.4, s32[512]{0:T(512)S(1)} %iota.17), dimensions={0}, to_apply=%region_1.2 | sort | flops 4608 | bytes 8192 | tf_op jit(solution)/shard_map/jit(argsort)/sort | solution.py:24
  49.2 15.2 %all-to-all-done.1 = bf16[128,4,1024]{2,1,0:T(4,128)(2,1)S(1)} async-done(((bf16[128,4,1024]{2,1,0:T(4,128)(2,1)}), bf16[128,4,1024]{2,1,0:T(4,128)(2,1)S(1)}, u32[]{:S(2)}, u32[]{:S(2)}) %all-to-all-start.1) | async-done | bytes 1048608 | tf_op jit(solution)/shard_map/all_to_all | solution.py:22
  64.4 0.3 reshape.73
  64.7 2.8 gather_fusion.2
  67.6 0.1 reshape.102
  67.7 0.1 iota_compare_fusion
  67.8 88.4 %all-gather.3.cloned.1.call-done = bf16[8192,1024]{1,0:T(8,128)(2,1)} async-done(((bf16[512,1024]{1,0:T(8,128)(2,1)}), bf16[8192,1024]{1,0:T(8,128)(2,1)}) %all-gather.3.cloned.1.call-update) | async-done | bytes 16777232 | tf_op jit(solution)/shard_map/all_gather | solution.py:33
  156.2 13.5 %gather_fusion.3 = bf16[64,128,1024]{2,1,0:T(8,128)(2,1)} fusion(bf16[64,128,1024]{2,1,0:T(8,128)(2,1)} %bitcast.13, s32[1024]{0:T(1024)S(1)} %pad_clamp_fusion), kind=kCustom, calls=%fused_computation.3 | custom fusion | bytes 33554688 | tf_op jit(solution)/shard_map/gather | solution.py:37
  169.7 7.3 %bitcast_convert_fusion = bf16[4,128,1024]{2,1,0:T(8,128)(2,1)S(1)} fusion(bf16[4,16,128,1024]{3,2,1,0:T(8,128)(2,1)} %bitcast.12, bf16[4,16,128,128]{3,2,1,0:T(8,128)(2,1)S(1)} %copy-done.1, pred[4,16]{1,0:T(4,128)(4,1)S(1)} %iota_compare_fusion), kind=kOutput, calls=%fused_computation.4 | convolution fusion | flops 2149056512 | bytes 19923008 | tf_op jit(solution)/shard_map/tkij,tkjf->tif/dot_general | solution.py:38
  177.0 1.6 multiply_convert_fusion.1
  178.7 2.2 fusion.6
  180.9 151.0 %all-reduce.2.cloned.1.call-done = f32[1024,512]{1,0:T(8,128)} async-done(((f32[1024,512]{1,0:T(8,128)}), f32[1024,512]{1,0:T(8,128)}) %all-reduce.2.cloned.1.call-update) | async-done | bytes 2097168 | tf_op jit(solution)/shard_map/psum | solution.py:46
  332.0 3.1 copy.12
  (26 shorter events, 0.2 us)
Async XLA Ops:
  7.2 30.5 %copy-start = (bf16[512,1024]{1,0:T(8,128)(2,1)S(1)}, bf16[512,1024]{1,0:T(8,128)(2,1)}, u32[]{:S(2)}) copy-start(bf16[512,1024]{1,0:T(8,128)(2,1)} %param.7) | copy-start | bytes 3145732
  41.0 23.5 %all-to-all-start.1 = ((bf16[128,4,1024]{2,1,0:T(4,128)(2,1)}), bf16[128,4,1024]{2,1,0:T(4,128)(2,1)S(1)}, u32[]{:S(2)}, u32[]{:S(2)}) async-start(bf16[128,4,1024]{2,1,0:T(4,128)(2,1)} %reshape.72), calls=%async_computation.1 | async-start | bytes 2097152 | tf_op jit(solution)/shard_map/all_to_all | solution.py:22
  45.4 110.8 %all-gather.3.cloned.1.call-start = ((), (), s32[]{:S(2)}) async-start(), calls=%async_computation.3 | async-start | bytes 17825792 | tf_op jit(solution)/shard_map/all_gather | solution.py:33
  64.7 2.9 copy-start.2
  64.7 3.0 copy-start.5
  67.5 264.4 %all-reduce.2.cloned.1.call-start = ((), (), s32[]{:S(2)}) async-start(), calls=%async_computation.2 | async-start | bytes 4194304 | tf_op jit(solution)/shard_map/psum | solution.py:46
  156.2 13.5 %copy-start.1 = (bf16[4,16,128,128]{3,2,1,0:T(8,128)(2,1)S(1)}, bf16[4,16,128,128]{3,2,1,0:T(8,128)(2,1)}, u32[]{:S(2)}) copy-start(bf16[4,16,128,128]{3,2,1,0:T(8,128)(2,1)} %param.11) | copy-start | bytes 6291460
  169.7 7.3 %copy-start.3 = (bf16[1024,512]{1,0:T(8,128)(2,1)S(1)}, bf16[1024,512]{1,0:T(8,128)(2,1)}, u32[]{:S(2)}) copy-start(bf16[1024,512]{1,0:T(8,128)(2,1)} %param.12) | copy-start | bytes 3145732
  177.0 1.7 copy-start.4
Sparse Core Ops, SparseCore 0:
  67.6 88.4 all-gather.2
  181.0 150.8 all-reduce.1

commit v2 on v1

v2 whole, which is shorter than its diff:
```python
import jax
import jax.numpy as jnp
from jax import lax
from jax.experimental import pallas as pl
from jax.experimental.pallas import tpu as pltpu
from jax.sharding import PartitionSpec as P

AXES = ("grp", "dom")


def regroup(features, node_order):
    row_count, width_in = features.shape
    devices = lax.axis_size("grp") * lax.axis_size("dom")
    per_pair = row_count // devices
    source_device = node_order // row_count
    source_row = node_order % row_count
    ordering = jnp.argsort(source_device, stable=True)
    requests = source_row[ordering].reshape(devices, per_pair)
    asked_rows = lax.all_to_all(requests, AXES, split_axis=0, concat_axis=0, tiled=True)
    outgoing = features[asked_rows.reshape(-1)].reshape(devices, per_pair, width_in)
    arrived = lax.all_to_all(outgoing, AXES, split_axis=0, concat_axis=0, tiled=True)
    arrived = arrived.reshape(row_count, width_in)
    inverse = jnp.argsort(ordering)
    return arrived[inverse]


def local_kernel(cols, count, panel, vals, weight, cot, hidden, term, chosen, acc, mixed, sems):
    tiles, blocks, size, _ = vals.shape

    def fetch(t, k):
        return pltpu.make_async_copy(panel.at[cols[t, k]], chosen.at[t, k], sems.at[t, k])

    for t in range(tiles):
        @pl.loop(0, count[t])
        def _(k):
            fetch(t, k).start()

    for t in range(tiles):
        live = count[t]
        fetch(t, 0).wait()
        acc[...] = jnp.dot(vals[t, 0], chosen[t, 0], preferred_element_type=jnp.float32)

        @pl.loop(1, live)
        def _(k):
            fetch(t, k).wait()
            acc[...] += jnp.dot(vals[t, k], chosen[t, k], preferred_element_type=jnp.float32)

        mixed[pl.ds(t * size, size), :] = acc[...].astype(jnp.bfloat16)

    rows = mixed[...]
    aggregate = jnp.dot(rows, weight[...], preferred_element_type=jnp.float32)
    sig = jax.nn.sigmoid(aggregate)
    hidden[...] = (aggregate * sig).astype(hidden.dtype)
    slope = sig * (1.0 + aggregate * (1.0 - sig))
    grad_agg = (cot[...].astype(jnp.float32) * slope).astype(jnp.bfloat16)
    term[...] = lax.dot_general(
        rows, grad_agg, (((0,), (0,)), ((), ())), preferred_element_type=jnp.float32
    ).astype(term.dtype)


def local_pass(everyone, block_cols, block_count, block_vals, weight, cotangent):
    tiles, blocks, size, _ = block_vals.shape
    rows, hidden_units = cotangent.shape
    width_in = weight.shape[0]
    panel = everyone.reshape(-1, size, width_in)
    vmem = pl.BlockSpec(memory_space=pltpu.VMEM)
    smem = pl.BlockSpec(memory_space=pltpu.SMEM)
    return pl.pallas_call(
        local_kernel,
        out_shape=(
            jax.ShapeDtypeStruct((rows, hidden_units), jnp.bfloat16),
            jax.ShapeDtypeStruct((width_in, hidden_units), jnp.bfloat16),
        ),
        in_specs=[smem, smem, pl.BlockSpec(memory_space=pl.ANY), vmem, vmem, vmem],
        out_specs=(vmem, vmem),
        scratch_shapes=[
            pltpu.VMEM((tiles, blocks, size, width_in), jnp.bfloat16),
            pltpu.VMEM((size, width_in), jnp.float32),
            pltpu.VMEM((rows, width_in), jnp.bfloat16),
            pltpu.SemaphoreType.DMA((tiles, blocks)),
        ],
        name="local_pass",
    )(block_cols, block_count, panel, block_vals, weight, cotangent)


def sum_terms(term):
    devices = lax.axis_size("grp") * lax.axis_size("dom")
    width_in, hidden_units = term.shape
    share = width_in // devices
    pieces = lax.all_to_all(
        term.reshape(devices, share, hidden_units), AXES, split_axis=0, concat_axis=0, tiled=True
    )
    summed = jnp.sum(pieces.astype(jnp.float32), axis=0).astype(jnp.bfloat16)
    copies = jnp.broadcast_to(summed[None], (devices, share, hidden_units))
    whole = lax.all_to_all(copies, AXES, split_axis=0, concat_axis=0, tiled=True)
    return whole.reshape(width_in, hidden_units).astype(jnp.float32)


def shards(features, node_order, block_cols, block_count, block_vals, weight, cotangent):
    ordered = regroup(features, node_order)
    everyone = lax.all_gather(ordered, "dom", axis=0, tiled=True)
    hidden, term = local_pass(everyone, block_cols, block_count, block_vals, weight, cotangent)
    return (hidden, sum_terms(term))


def solution(mesh):
    placed = (
        P(AXES, None),
        P(AXES),
        P(AXES, None),
        P(AXES),
        P(AXES, None, None, None),
        P(),
        P(AXES, None),
    )
    return jax.shard_map(
        shards,
        mesh=mesh,
        in_specs=placed,
        out_specs=(P(AXES, None), P()),
        check_vma=False,
    )
```

time: 342 us -> 231 us (0.68)
  waiting for transfers between devices: 255 us -> 104 us
  blocking collectives: 20.9 us -> 77.6 us
  local copies, waits for them, and re-layouts: 27.2 us -> 10.6 us
  matrix products: 11.2 us -> 0 us
  Pallas kernels: 0 us -> 9.35 us
    psum x1 -> x0, waiting for transfers between devices: 151 us -> none  [shards(): grad_weight = lax.psum(local_grad, ('grp', 'dom'))]
    all_to_all x1 -> x3, blocking collectives: 20.9 us -> 77.6 us  [the longest x1 33.2 us: sum_terms(): lax.all_to_all(term.reshape(devices, share, hidden_units), AXES, split_ax...]
    gather x1 -> x0, local copies, waits for them, and re-layouts: 13.5 us -> none  [shards(): selected = panel_tiles[block_cols]]
    dot_general x3 -> x0, matrix products: 11.2 us -> none  [the longest x1 7.32 us: shards(): jnp.einsum('tkij,tkjf->tif', masked_vals, selected, preferred_element_typ...]
    pallas_call x0 -> x1, Pallas kernels: none -> 9.35 us  [local_pass(): pl.pallas_call(local_kernel, out_shape=(jax.ShapeDtypeStruct((rows, hidde...]
  transfers between devices with their start and end apart: 3 -> 2, of which waited for: 3 -> 2; matrix products, arithmetic and copies ran while one was open for 1% -> 2% of each run, Pallas kernels for 0% -> 0%
where the time goes in v2:
time: 231 us
  waiting for transfers between devices  104 us (45%)
  blocking collectives  77.6 us (34%)
  between operations  14.1 us (6%)
  other arithmetic  11 us (5%)
  local copies, waits for them, and re-layouts  10.6 us (5%)
  Pallas kernels  9.35 us (4%)
  starting transfers between devices  4.44 us (2%)
    all_gather x1, waiting for transfers between devices, shards(): everyone = lax.all_gather(ordered, 'dom', axis=0, tiled=True)  88.6 us
    all_to_all x1, blocking collectives, sum_terms(): lax.all_to_all(term.reshape(devices, share, hidden_units), AXES, split_ax...  33.2 us
    all_to_all x1, blocking collectives, sum_terms(): lax.all_to_all(copies, AXES, split_axis=0, concat_axis=0, tiled=True)  23.5 us
    all_to_all x1, blocking collectives, regroup(): lax.all_to_all(requests, AXES, split_axis=0, concat_axis=0, tiled=True)  20.9 us
    all_to_all x1, waiting for transfers between devices, regroup(): lax.all_to_all(outgoing, AXES, split_axis=0, concat_axis=0, tiled=True)  15.2 us
    pallas_call x1, Pallas kernels, local_pass(): pl.pallas_call(local_kernel, out_shape=(jax.ShapeDtypeStruct((rows, hidde...  9.35 us
  transfers between devices with their start and end apart: 2, of which 2 were waited for; matrix products, arithmetic and copies ran while one was open for 2% of the time, Pallas kernels for 0%

profile of v2, /device:TPU:1, one launch (start us, length us, event | category | flops | bytes accessed | tf_op | source)
XLA Modules:
  0.0 230.9 jit_solution(15623516986244785558)
XLA Ops:
  7.2 0.8 add_select_fusion
  8.0 3.8 %sort.34 = (s32[512]{0:T(512)}, s32[512]{0:T(512)S(1)}) sort(s32[512]{0:T(512)S(1)} %get-tuple-element.10, s32[512]{0:T(512)S(1)} %iota.8), dimensions={0}, to_apply=%region_0.1 | sort | flops 4608 | bytes 8192 | tf_op jit(solution)/shard_map/jit(argsort)/sort | solution.py:17
  11.7 3.5 %gather_fusion = s32[512]{0:T(512)S(1)} fusion(s32[512]{0:T(512)S(1)} %get-tuple-element.11, s32[1024]{0:T(1024)S(1)} %pad_clamp_fusion.2), kind=kCustom, calls=%fused_computation | custom fusion | bytes 6144 | tf_op jit(solution)/shard_map/gather | solution.py:18
  15.2 0.1 all_to_all.15
  15.4 20.9 %all_to_all.24 = s32[128,1,4]{2,1,0:T(1,128)S(1)} all-to-all(s32[128,1,4]{2,1,0:T(1,128)S(1)} %bitcast.9), channel_id=1, replica_groups=mesh['grp'=8,'dom'=16] {'grp','dom'}, dimensions={0} | all-to-all | bytes 4096 | tf_op jit(solution)/shard_map/all_to_all | solution.py:19
  36.2 0.5 broadcast.58
  36.7 0.8 reduce.4
  37.6 0.1 reshape.56
  37.7 2.1 gather_fusion.1
  39.8 1.2 reshape.57
  41.0 4.4 %all-to-all-start.1 = ((bf16[128,4,1024]{2,1,0:T(4,128)(2,1)}), bf16[128,4,1024]{2,1,0:T(4,128)(2,1)S(1)}, u32[]{:S(2)}, u32[]{:S(2)}) async-start(bf16[128,4,1024]{2,1,0:T(4,128)(2,1)} %reshape.57), calls=%async_computation.1 | async-start | bytes 2097152 | tf_op jit(solution)/shard_map/all_to_all | solution.py:21
  45.4 0.0 all-gather.3.cloned.1.call-start
  45.4 3.8 %sort.35 = (s32[512]{0:T(512)}, s32[512]{0:T(512)S(1)}) sort(s32[512]{0:T(512)S(1)} %get-tuple-element.6, s32[512]{0:T(512)S(1)} %iota.9), dimensions={0}, to_apply=%region_1.2 | sort | flops 4608 | bytes 8192 | tf_op jit(solution)/shard_map/jit(argsort)/sort | solution.py:23
  49.2 15.2 %all-to-all-done.1 = bf16[128,4,1024]{2,1,0:T(4,128)(2,1)S(1)} async-done(((bf16[128,4,1024]{2,1,0:T(4,128)(2,1)}), bf16[128,4,1024]{2,1,0:T(4,128)(2,1)S(1)}, u32[]{:S(2)}, u32[]{:S(2)}) %all-to-all-start.1) | async-done | bytes 1048608 | tf_op jit(solution)/shard_map/all_to_all | solution.py:21
  64.4 0.3 reshape.58
  64.7 2.8 %gather_fusion.2 = bf16[512,1024]{1,0:T(8,128)(2,1)} fusion(bf16[512,1024]{1,0:T(8,128)(2,1)S(1)} %reshape.58, s32[1024]{0:T(1024)S(1)} %pad_clamp_fusion), kind=kCustom, calls=%fused_computation.2 | custom fusion | bytes 2099200 | tf_op jit(solution)/shard_map/gather | solution.py:24
  67.5 0.0 all-gather.3.cloned.1.call-update
  67.5 88.6 %all-gather.3.cloned.1.call-done = bf16[8192,1024]{1,0:T(8,128)(2,1)} async-done(((bf16[512,1024]{1,0:T(8,128)(2,1)}), bf16[8192,1024]{1,0:T(8,128)(2,1)}) %all-gather.3.cloned.1.call-update) | async-done | bytes 16777232 | tf_op jit(solution)/shard_map/all_gather | solution.py:101
  156.1 9.3 %local_pass.1 = (bf16[512,512]{1,0:T(8,128)(2,1)}, bf16[1024,512]{1,0:T(8,128)(2,1)}) custom-call(s32[4,16]{1,0:T(4,128)} %cols.1, s32[4]{0:T(128)} %count.1, bf16[64,128,1024]{2,1,0:T(8,128)(2,1)} %bitcast.7, bf16[4,16,128,128]{3,2,1,0:T(8,128)(2,1)} %vals.1, bf16[1024,512]{1,0:T(8,128)(2,1)} %weight.1, bf16[512,512]{1,0:T(8,128)(2,1)} %cot.1), custom_call_target="tpu_custom_call" | custom-call | tf_op jit(solution)/shard_map/local_pass/pallas_call | solution.py:68
  165.5 33.2 %all_to_all.25 = bf16[128,8,512]{2,1,0:T(8,128)(2,1)S(1)} all-to-all(bf16[128,8,512]{2,1,0:T(8,128)(2,1)} %bitcast.8), channel_id=1, replica_groups=mesh['grp'=8,'dom'=16] {'grp','dom'}, dimensions={0} | all-to-all | bytes 2097152 | tf_op jit(solution)/shard_map/all_to_all | solution.py:90
  198.7 0.2 reduce_sum.12
  198.8 0.1 broadcast_in_dim.15
  198.9 23.5 %all_to_all.26 = bf16[128,8,512]{2,1,0:T(8,128)(2,1)S(1)} all-to-all(bf16[128,8,512]{2,1,0:T(8,128)(2,1)S(1)} %broadcast_in_dim.15), channel_id=1, replica_groups=mesh['grp'=8,'dom'=16] {'grp','dom'}, dimensions={0} | all-to-all | bytes 2097152 | tf_op jit(solution)/shard_map/all_to_all | solution.py:95
  222.5 1.6 bitcast_convert_fusion
  (10 shorter events, 0.0 us)
Async XLA Ops:
  7.2 30.5 %copy-start = (bf16[512,1024]{1,0:T(8,128)(2,1)S(1)}, bf16[512,1024]{1,0:T(8,128)(2,1)}, u32[]{:S(2)}) copy-start(bf16[512,1024]{1,0:T(8,128)(2,1)} %param.7) | copy-start | bytes 3145732
  41.0 23.5 %all-to-all-start.1 = ((bf16[128,4,1024]{2,1,0:T(4,128)(2,1)}), bf16[128,4,1024]{2,1,0:T(4,128)(2,1)S(1)}, u32[]{:S(2)}, u32[]{:S(2)}) async-start(bf16[128,4,1024]{2,1,0:T(4,128)(2,1)} %reshape.57), calls=%async_computation.1 | async-start | bytes 2097152 | tf_op jit(solution)/shard_map/all_to_all | solution.py:21
  45.4 110.7 %all-gather.3.cloned.1.call-start = ((), (), s32[]{:S(2)}) async-start(), calls=%async_computation.4 | async-start | bytes 17825792 | tf_op jit(solution)/shard_map/all_gather | solution.py:101
Sparse Core Ops, SparseCore 0:
  67.6 88.4 all-gather.2

commit v3 on v2

--- a/solution.py
+++ b/solution.py
@@ -22,6 +22,142 @@
     arrived = arrived.reshape(row_count, width_in)
     inverse = jnp.argsort(ordering)
     return arrived[inverse]
+
+
+def piece_plan(rows):
+    half = rows // 2
+    cut = rows * 11 // 32
+    upper = rows - cut
+    up = [
+        (0, -1, 0, half, None), (0, -1, half, rows, None), (0, 2, 0, half, ("up", 0)),
+        (1, -1, 0, cut, ("side", 0)), (1, 2, cut, half, ("side", 2)), (1, 2, 0, cut, ("up", 3)),
+    ]
+    down = [
+        (0, 1, half, rows, None), (0, 1, 0, half, None), (0, 2, half, rows, ("down", 0)),
+        (1, 1, upper, rows, ("side", 1)), (1, 2, half, upper, ("side", 3)), (1, 2, upper, rows, ("down", 3)),
+    ]
+    side = [
+        (1, 0, 0, half, None), (1, 0, half, rows, None), (1, -1, cut, half, ("up", 0)),
+        (1, 1, half, upper, ("down", 0)), (1, -1, half, rows, ("up", 1)), (1, 1, 0, half, ("down", 1)),
+    ]
+    return {"up": up, "down": down, "side": side}
+
+
+ARRIVALS = (
+    ("up", 0), ("down", 0), ("side", 0), ("up", 1), ("down", 1), ("side", 1), ("side", 2), ("side", 3),
+    ("up", 2), ("down", 2), ("side", 4), ("up", 3), ("down", 3), ("up", 4), ("down", 4), ("side", 5),
+    ("up", 5), ("down", 5),
+)
+LINKS = ("up", "down", "side")
+
+
+def gather_kernel(own, out, send_sems, recv_sems, pass_send, pass_recv, keep_sem):
+    rows = own.shape[0]
+    me = lax.axis_index("dom")
+    depth, column, core = me // 4, (me // 2) % 2, me % 2
+
+    def place(other_column, shift, which_core):
+        z = lax.rem(depth + shift + 4, 4)
+        x = column + other_column * (1 - 2 * column)
+        return z * 4 + x * 2 + which_core
+
+    partner = place(0, 0, 1 - core)
+    targets = {"up": place(0, 1, core), "down": place(0, -1, core), "side": place(1, 0, core)}
+
+    barrier = pltpu.get_barrier_semaphore()
+    for target in (*targets.values(), partner):
+        pl.semaphore_signal(barrier, inc=1, device_id={"dom": target}, device_id_type=pl.DeviceIdType.MESH)
+    keep = pltpu.make_async_copy(own, out.at[me], keep_sem)
+    keep.start()
+    pl.semaphore_wait(barrier, 4)
+
+    plan = piece_plan(rows)
+    moved = {"up": (0, 1), "down": (0, -1), "side": (1, 0)}
+
+    def send(link, number):
+        other, shift, low, high, _ = plan[link][number]
+        jump, step = moved[link]
+        span = pl.ds(low, high - low)
+        source_other, source_shift = (other + jump) % 2, shift + step
+        owner = place(source_other, source_shift, core)
+        slot = LINKS.index(link) * 6 + number
+        block = own.at[span] if plan[link][number][4] is None else out.at[owner, span]
+        return pltpu.make_async_remote_copy(
+            src_ref=block, dst_ref=out.at[owner, span],
+            send_sem=send_sems.at[slot], recv_sem=recv_sems.at[slot],
+            device_id={"dom": targets[link]}, device_id_type=pl.DeviceIdType.MESH,
+        )
+
+    def landed(link, number):
+        other, shift, low, high, _ = plan[link][number]
+        span = pl.ds(low, high - low)
+        slot = LINKS.index(link) * 6 + number
+        here = out.at[place(other, shift, core), span]
+        return pltpu.make_async_remote_copy(
+            src_ref=here, dst_ref=here,
+            send_sem=send_sems.at[slot], recv_sem=recv_sems.at[slot],
+            device_id={"dom": targets[link]}, device_id_type=pl.DeviceIdType.MESH,
+        )
+
+    def hand_over(number, block, there):
+        return pltpu.make_async_remote_copy(
+            src_ref=block, dst_ref=there,
+            send_sem=pass_send.at[number], recv_sem=pass_recv.at[number],
+            device_id={"dom": partner}, device_id_type=pl.DeviceIdType.MESH,
+        )
+
+    sent = []
+    for number in range(2):
+        for link in LINKS:
+            copy = send(link, number)
+            copy.start()
+            sent.append(copy)
+    copy = hand_over(18, own, out.at[me])
+    copy.start()
+    sent.append(copy)
+
+    for order, (link, number) in enumerate(ARRIVALS):
+        landed(link, number).wait_recv()
+        for onward in LINKS:
+            for later in range(2, 6):
+                if plan[onward][later][4] == (link, number):
+                    copy = send(onward, later)
+                    copy.start()
+                    sent.append(copy)
+        other, shift, low, high, _ = plan[link][number]
+        here = out.at[place(other, shift, core), pl.ds(low, high - low)]
+        copy = hand_over(order, here, here)
+        copy.start()
+        sent.append(copy)
+
+    hand_over(18, own, out.at[partner]).wait_recv()
+    for order, (link, number) in enumerate(ARRIVALS):
+        other, shift, low, high, _ = plan[link][number]
+        there = out.at[place(other, shift, 1 - core), pl.ds(low, high - low)]
+        hand_over(order, there, there).wait_recv()
+    for copy in sent:
+        copy.wait_send()
+    keep.wait()
+
+
+def gather_group(ordered):
+    rows, width_in = ordered.shape
+    group = lax.axis_size("dom")
+    return pl.pallas_call(
+        gather_kernel,
+        out_shape=jax.ShapeDtypeStruct((group, rows, width_in), ordered.dtype),
+        in_specs=[pl.BlockSpec(memory_space=pltpu.VMEM)],
+        out_specs=pl.BlockSpec(memory_space=pl.ANY),
+        scratch_shapes=[
+            pltpu.SemaphoreType.DMA((18,)),
+            pltpu.SemaphoreType.DMA((18,)),
+            pltpu.SemaphoreType.DMA((19,)),
+            pltpu.SemaphoreType.DMA((19,)),
+            pltpu.SemaphoreType.DMA,
+        ],
+        compiler_params=pltpu.CompilerParams(collective_id=0, has_side_effects=True),
+        name="gather_group",
+    )(ordered)
 
 
 def local_kernel(cols, count, panel, vals, weight, cot, hidden, term, chosen, acc, mixed, sems):
@@ -98,7 +234,7 @@
 
 def shards(features, node_order, block_cols, block_count, block_vals, weight, cotangent):
     ordered = regroup(features, node_order)
-    everyone = lax.all_gather(ordered, "dom", axis=0, tiled=True)
+    everyone = gather_group(ordered)
     hidden, term = local_pass(everyone, block_cols, block_count, block_vals, weight, cotangent)
     return (hidden, sum_terms(term))
 

time: 231 us -> 188 us (0.81)
  waiting for transfers between devices: 104 us -> 15.3 us
  Pallas kernels: 9.35 us -> 70.9 us
  between operations: 14.1 us -> 0.74 us
  blocking collectives: 77.6 us -> 74.7 us
    all_gather x1 -> x0, waiting for transfers between devices: 88.6 us -> none  [shards(): everyone = lax.all_gather(ordered, 'dom', axis=0, tiled=True)]
    pallas_call x0 -> x1, Pallas kernels: none -> 61.1 us  [gather_group(): pl.pallas_call(gather_kernel, out_shape=jax.ShapeDtypeStruct((group, rows...]
    all_to_all x1, blocking collectives: 33.2 us -> 30.3 us  [sum_terms(): lax.all_to_all(term.reshape(devices, share, hidden_units), AXES, split_ax...]
  transfers between devices with their start and end apart: 2 -> 1, of which waited for: 2 -> 1; matrix products, arithmetic and copies ran while one was open for 2% -> 2% of each run, Pallas kernels for 0% -> 0%
where the time goes in v3:
time: 188 us; the launch traced here: 187 us
  blocking collectives  74.7 us (40%)
  Pallas kernels  70.9 us (38%)
  waiting for transfers between devices  15.3 us (8%)
  other arithmetic  11 us (6%)
  local copies, waits for them, and re-layouts  10.6 us (6%)
  starting transfers between devices  4.39 us (2%)
    pallas_call x1, Pallas kernels, gather_group(): pl.pallas_call(gather_kernel, out_shape=jax.ShapeDtypeStruct((group, rows...  61.1 us
    all_to_all x1, blocking collectives, sum_terms(): lax.all_to_all(term.reshape(devices, share, hidden_units), AXES, split_ax...  30.3 us
    all_to_all x1, blocking collectives, sum_terms(): lax.all_to_all(copies, AXES, split_axis=0, concat_axis=0, tiled=True)  23.5 us
    all_to_all x1, blocking collectives, regroup(): lax.all_to_all(requests, AXES, split_axis=0, concat_axis=0, tiled=True)  20.9 us
    all_to_all x1, waiting for transfers between devices, regroup(): lax.all_to_all(outgoing, AXES, split_axis=0, concat_axis=0, tiled=True)  15.3 us
    pallas_call x1, Pallas kernels, local_pass(): pl.pallas_call(local_kernel, out_shape=(jax.ShapeDtypeStruct((rows, hidde...  9.79 us
    all_to_all x1, starting transfers between devices, regroup(): lax.all_to_all(outgoing, AXES, split_axis=0, concat_axis=0, tiled=True)  4.39 us
    sort x1, other arithmetic, regroup(): ordering = jnp.argsort(source_device, stable=True)  3.77 us
  transfers between devices with their start and end apart: 1, of which 1 were waited for; matrix products, arithmetic and copies ran while one was open for 2% of the time, Pallas kernels for 0%

profile of v3, /device:TPU:1, one launch (start us, length us, event | category | flops | bytes accessed | tf_op | source)
XLA Modules:
  0.0 187.5 jit_solution(1136689910570965566)
XLA Ops:
  0.6 0.0 copy-start
  0.6 0.8 add_select_fusion
  1.4 3.8 %sort.34 = (s32[512]{0:T(512)}, s32[512]{0:T(512)S(1)}) sort(s32[512]{0:T(512)S(1)} %get-tuple-element.10, s32[512]{0:T(512)S(1)} %iota.8), dimensions={0}, to_apply=%region_0.1 | sort | flops 4608 | bytes 8192 | tf_op jit(solution)/shard_map/jit(argsort)/sort | solution.py:17
  5.2 3.5 %gather_fusion = s32[512]{0:T(512)S(1)} fusion(s32[512]{0:T(512)S(1)} %get-tuple-element.11, s32[1024]{0:T(1024)S(1)} %pad_clamp_fusion.2), kind=kCustom, calls=%fused_computation | custom fusion | bytes 6144 | tf_op jit(solution)/shard_map/gather | solution.py:18
  8.7 0.1 all_to_all.15
  8.8 20.9 %all_to_all.24 = s32[128,1,4]{2,1,0:T(1,128)S(1)} all-to-all(s32[128,1,4]{2,1,0:T(1,128)S(1)} %bitcast.9), channel_id=1, replica_groups=mesh['grp'=8,'dom'=16] {'grp','dom'}, dimensions={0} | all-to-all | bytes 4096 | tf_op jit(solution)/shard_map/all_to_all | solution.py:19
  29.7 0.5 broadcast.58
  30.2 0.8 reduce.4
  31.0 0.1 reshape.56
  31.2 0.0 copy-done
  31.2 2.1 %gather_fusion.1 = bf16[512,1024]{1,0:T(8,128)(2,1)S(1)} fusion(bf16[512,1024]{1,0:T(8,128)(2,1)S(1)} %copy-done, s32[1024]{0:T(1024)S(1)} %pad_clamp_fusion.1), kind=kCustom, calls=%fused_computation.1 | custom fusion | bytes 2099200 | tf_op jit(solution)/shard_map/gather | solution.py:20
  33.2 1.2 reshape.57
  34.4 4.4 %all-to-all-start.1 = ((bf16[128,4,1024]{2,1,0:T(4,128)(2,1)}), bf16[128,4,1024]{2,1,0:T(4,128)(2,1)S(1)}, u32[]{:S(2)}, u32[]{:S(2)}) async-start(bf16[128,4,1024]{2,1,0:T(4,128)(2,1)} %reshape.57), calls=%async_computation.1 | async-start | bytes 2097152 | tf_op jit(solution)/shard_map/all_to_all | solution.py:21
  38.9 3.8 %sort.35 = (s32[512]{0:T(512)}, s32[512]{0:T(512)S(1)}) sort(s32[512]{0:T(512)S(1)} %get-tuple-element.6, s32[512]{0:T(512)S(1)} %iota.9), dimensions={0}, to_apply=%region_1.2 | sort | flops 4608 | bytes 8192 | tf_op jit(solution)/shard_map/jit(argsort)/sort | solution.py:23
  42.6 15.3 %all-to-all-done.1 = bf16[128,4,1024]{2,1,0:T(4,128)(2,1)S(1)} async-done(((bf16[128,4,1024]{2,1,0:T(4,128)(2,1)}), bf16[128,4,1024]{2,1,0:T(4,128)(2,1)S(1)}, u32[]{:S(2)}, u32[]{:S(2)}) %all-to-all-start.1) | async-done | bytes 1048608 | tf_op jit(solution)/shard_map/all_to_all | solution.py:21
  57.9 0.3 reshape.58
  58.2 2.8 %gather_fusion.2 = bf16[512,1024]{1,0:T(8,128)(2,1)} fusion(bf16[512,1024]{1,0:T(8,128)(2,1)S(1)} %reshape.58, s32[1024]{0:T(1024)S(1)} %pad_clamp_fusion), kind=kCustom, calls=%fused_computation.2 | custom fusion | bytes 2099200 | tf_op jit(solution)/shard_map/gather | solution.py:24
  60.9 61.1 %gather_group.1 = bf16[16,512,1024]{2,1,0:T(8,128)(2,1)} custom-call(bf16[512,1024]{1,0:T(8,128)(2,1)} %gather_fusion.2), custom_call_target="tpu_custom_call" | custom-call | tf_op jit(solution)/shard_map/gather_group/pallas_call | solution.py:146
  122.0 9.8 %local_pass.1 = (bf16[512,512]{1,0:T(8,128)(2,1)}, bf16[1024,512]{1,0:T(8,128)(2,1)}) custom-call(s32[4,16]{1,0:T(4,128)} %cols.1, s32[4]{0:T(128)} %count.1, bf16[64,128,1024]{2,1,0:T(8,128)(2,1)} %bitcast.7, bf16[4,16,128,128]{3,2,1,0:T(8,128)(2,1)} %vals.1, bf16[1024,512]{1,0:T(8,128)(2,1)} %weight.1, bf16[512,512]{1,0:T(8,128)(2,1)} %cot.1), custom_call_target="tpu_custom_call" | custom-call | tf_op jit(solution)/shard_map/local_pass/pallas_call | solution.py:204
  131.8 30.3 %all_to_all.25 = bf16[128,8,512]{2,1,0:T(8,128)(2,1)S(1)} all-to-all(bf16[128,8,512]{2,1,0:T(8,128)(2,1)} %bitcast.8), channel_id=1, replica_groups=mesh['grp'=8,'dom'=16] {'grp','dom'}, dimensions={0} | all-to-all | bytes 2097152 | tf_op jit(solution)/shard_map/all_to_all | solution.py:226
  162.1 0.2 reduce_sum.12
  162.3 0.1 broadcast_in_dim.15
  162.3 23.5 %all_to_all.26 = bf16[128,8,512]{2,1,0:T(8,128)(2,1)S(1)} all-to-all(bf16[128,8,512]{2,1,0:T(8,128)(2,1)S(1)} %broadcast_in_dim.15), channel_id=1, replica_groups=mesh['grp'=8,'dom'=16] {'grp','dom'}, dimensions={0} | all-to-all | bytes 2097152 | tf_op jit(solution)/shard_map/all_to_all | solution.py:231
  185.9 1.6 bitcast_convert_fusion
  (8 shorter events, 0.0 us)
Async XLA Ops:
  0.6 30.5 %copy-start = (bf16[512,1024]{1,0:T(8,128)(2,1)S(1)}, bf16[512,1024]{1,0:T(8,128)(2,1)}, u32[]{:S(2)}) copy-start(bf16[512,1024]{1,0:T(8,128)(2,1)} %param.7) | copy-start | bytes 3145732
  34.4 23.5 %all-to-all-start.1 = ((bf16[128,4,1024]{2,1,0:T(4,128)(2,1)}), bf16[128,4,1024]{2,1,0:T(4,128)(2,1)S(1)}, u32[]{:S(2)}, u32[]{:S(2)}) async-start(bf16[128,4,1024]{2,1,0:T(4,128)(2,1)} %reshape.57), calls=%async_computation.1 | async-start | bytes 2097152 | tf_op jit(solution)/shard_map/all_to_all | solution.py:21

commit v4 on v3

--- a/solution.py
+++ b/solution.py
@@ -189,9 +189,12 @@
     hidden[...] = (aggregate * sig).astype(hidden.dtype)
     slope = sig * (1.0 + aggregate * (1.0 - sig))
     grad_agg = (cot[...].astype(jnp.float32) * slope).astype(jnp.bfloat16)
-    term[...] = lax.dot_general(
+    products = lax.dot_general(
         rows, grad_agg, (((0,), (0,)), ((), ())), preferred_element_type=jnp.float32
     ).astype(term.dtype)
+    columns = term.shape[2]
+    for side in range(2):
+        term[side] = products[:, side * columns:(side + 1) * columns]
 
 
 def local_pass(everyone, block_cols, block_count, block_vals, weight, cotangent):
@@ -205,7 +208,7 @@
         local_kernel,
         out_shape=(
             jax.ShapeDtypeStruct((rows, hidden_units), jnp.bfloat16),
-            jax.ShapeDtypeStruct((width_in, hidden_units), jnp.bfloat16),
+            jax.ShapeDtypeStruct((2, width_in, hidden_units // 2), jnp.bfloat16),
         ),
         in_specs=[smem, smem, pl.BlockSpec(memory_space=pl.ANY), vmem, vmem, vmem],
         out_specs=(vmem, vmem),
@@ -219,17 +222,106 @@
     )(block_cols, block_count, panel, block_vals, weight, cotangent)
 
 
+def sum_kernel(term, total, paired, half, pieces, chunk, whole, pair_sems, out_sems, in_sems):
+    chips = term.shape[1]
+    grp, dom = lax.axis_index("grp"), lax.axis_index("dom")
+    core = dom % 2
+    chip = grp * 8 + dom // 2
+    mesh_ids = pl.DeviceIdType.MESH
+    partner = {"grp": grp, "dom": dom + 1 - 2 * core}
+
+    def ahead(offset):
+        x_hi, y = lax.rem(grp // 4 + offset // 32, 2), lax.rem(grp % 4 + (offset // 8) % 4, 4)
+        z, x_lo = lax.rem(dom // 4 + (offset // 2) % 4, 4), lax.rem((dom // 2) % 2 + offset % 2, 2)
+        return {"grp": x_hi * 4 + y, "dom": z * 4 + x_lo * 2 + core}
+
+    barrier = pltpu.get_barrier_semaphore()
+    pl.semaphore_signal(barrier, inc=1, device_id=partner, device_id_type=mesh_ids)
+
+    @pl.loop(1, chips)
+    def _(offset):
+        pl.semaphore_signal(barrier, inc=1, device_id=ahead(offset), device_id_type=mesh_ids)
+
+    pl.semaphore_wait(barrier, chips)
+
+    swap = pltpu.make_async_remote_copy(
+        src_ref=term.at[1 - core], dst_ref=paired, send_sem=pair_sems.at[0], recv_sem=pair_sems.at[1],
+        device_id=partner, device_id_type=mesh_ids,
+    )
+    swap.start()
+    swap.wait()
+    half[...] = (term[core].astype(jnp.float32) + paired[...].astype(jnp.float32)).astype(half.dtype)
+
+    def place(offset):
+        to = ahead(offset)
+        return to["grp"] * 8 + to["dom"] // 2
+
+    @pl.loop(1, chips)
+    def _(offset):
+        pltpu.make_async_remote_copy(
+            src_ref=half.at[place(offset)], dst_ref=pieces.at[offset - 1],
+            send_sem=out_sems.at[0], recv_sem=in_sems.at[0],
+            device_id=ahead(offset), device_id_type=mesh_ids,
+        ).start()
+
+    def all_pieces(number):
+        return pltpu.make_async_remote_copy(
+            src_ref=pieces, dst_ref=pieces, send_sem=out_sems.at[number], recv_sem=in_sems.at[number],
+            device_id=partner, device_id_type=mesh_ids,
+        )
+
+    all_pieces(0).wait_recv()
+    summed = half[chip].astype(jnp.float32) + jnp.sum(pieces[...].astype(jnp.float32), axis=0)
+    chunk[...] = summed.astype(chunk.dtype)
+    all_pieces(0).wait_send()
+
+    @pl.loop(1, chips)
+    def _(offset):
+        pltpu.make_async_remote_copy(
+            src_ref=chunk, dst_ref=whole.at[core, chip],
+            send_sem=out_sems.at[1], recv_sem=in_sems.at[1],
+            device_id=ahead(offset), device_id_type=mesh_ids,
+        ).start()
+
+    whole[core, chip] = chunk[...]
+    all_pieces(1).wait_recv()
+    give = pltpu.make_async_remote_copy(
+        src_ref=whole.at[core], dst_ref=whole.at[core], send_sem=pair_sems.at[2], recv_sem=pair_sems.at[3],
+        device_id=partner, device_id_type=mesh_ids,
+    )
+    give.start()
+    total[core] = whole[core]
+    give.wait()
+    total[1 - core] = whole[1 - core]
+    all_pieces(1).wait_send()
+
+
 def sum_terms(term):
-    devices = lax.axis_size("grp") * lax.axis_size("dom")
-    width_in, hidden_units = term.shape
-    share = width_in // devices
-    pieces = lax.all_to_all(
-        term.reshape(devices, share, hidden_units), AXES, split_axis=0, concat_axis=0, tiled=True
-    )
-    summed = jnp.sum(pieces.astype(jnp.float32), axis=0).astype(jnp.bfloat16)
-    copies = jnp.broadcast_to(summed[None], (devices, share, hidden_units))
-    whole = lax.all_to_all(copies, AXES, split_axis=0, concat_axis=0, tiled=True)
-    return whole.reshape(width_in, hidden_units).astype(jnp.float32)
+    chips = lax.axis_size("grp") * lax.axis_size("dom") // 2
+    _, width_in, columns = term.shape
+    share = width_in // chips
+    shape = (2, chips, share, columns)
+    vmem = pl.BlockSpec(memory_space=pltpu.VMEM)
+    whole = pl.pallas_call(
+        sum_kernel,
+        out_shape=jax.ShapeDtypeStruct(shape, term.dtype),
+        in_specs=[vmem],
+        out_specs=vmem,
+        scratch_shapes=[
+            pltpu.VMEM(shape[1:], term.dtype),
+            pltpu.VMEM(shape[1:], term.dtype),
+            pltpu.VMEM((chips - 1, share, columns), term.dtype),
+            pltpu.VMEM((share, columns), term.dtype),
+            pltpu.VMEM(shape, term.dtype),
+            pltpu.SemaphoreType.DMA((4,)),
+            pltpu.SemaphoreType.DMA((2,)),
+            pltpu.SemaphoreType.DMA((2,)),
+        ],
+        compiler_params=pltpu.CompilerParams(collective_id=1, has_side_effects=True),
+        name="sum_terms",
+    )(term.reshape(shape))
+    sides = whole.reshape(2, width_in, columns).astype(jnp.float32)
+    return jnp.concatenate([sides[0], sides[1]], axis=1)
 
 
 def shards(features, node_order, block_cols, block_count, block_vals, weight, cotangent):

time: 188 us -> 174 us (0.926)
  blocking collectives: 74.7 us -> 20.9 us
  Pallas kernels: 70.9 us -> 109 us
    all_to_all x2 -> x0, blocking collectives: 53.8 us -> none  [the longest x1 30.3 us: sum_terms(): lax.all_to_all(term.reshape(devices, share, hidden_units), AXES, split_ax...]
    pallas_call x0 -> x1, Pallas kernels: none -> 37.3 us  [sum_terms(): pl.pallas_call(sum_kernel, out_shape=jax.ShapeDtypeStruct(shape, term.dty...]
where the time goes in v4:
time: 174 us
  Pallas kernels  109 us (63%)
  blocking collectives  20.9 us (12%)
  waiting for transfers between devices  15.3 us (9%)
  local copies, waits for them, and re-layouts  12 us (7%)
  other arithmetic  10.8 us (6%)
  starting transfers between devices  4.39 us (3%)
    pallas_call x1, Pallas kernels, gather_group(): pl.pallas_call(gather_kernel, out_shape=jax.ShapeDtypeStruct((group, rows...  61.1 us
    pallas_call x1, Pallas kernels, sum_terms(): pl.pallas_call(sum_kernel, out_shape=jax.ShapeDtypeStruct(shape, term.dty...  37.3 us
    all_to_all x1, blocking collectives, regroup(): lax.all_to_all(requests, AXES, split_axis=0, concat_axis=0, tiled=True)  20.9 us
    all_to_all x1, waiting for transfers between devices, regroup(): lax.all_to_all(outgoing, AXES, split_axis=0, concat_axis=0, tiled=True)  15.3 us
    pallas_call x1, Pallas kernels, local_pass(): pl.pallas_call(local_kernel, out_shape=(jax.ShapeDtypeStruct((rows, hidde...  11.1 us
    all_to_all x1, starting transfers between devices, regroup(): lax.all_to_all(outgoing, AXES, split_axis=0, concat_axis=0, tiled=True)  4.39 us
    sort x1, other arithmetic, regroup(): ordering = jnp.argsort(source_device, stable=True)  3.77 us
    sort x1, other arithmetic, regroup(): inverse = jnp.argsort(ordering)  3.77 us
  transfers between devices with their start and end apart: 1, of which 1 were waited for; matrix products, arithmetic and copies ran while one was open for 2% of the time, Pallas kernels for 0%

profile of v4, /device:TPU:1, one launch (start us, length us, event | category | flops | bytes accessed | tf_op | source)
XLA Modules:
  0.0 173.5 jit_solution(30018480979341866)
XLA Ops:
  0.6 0.0 copy-start
  0.6 0.8 add_select_fusion
  1.4 3.8 %sort.34 = (s32[512]{0:T(512)}, s32[512]{0:T(512)S(1)}) sort(s32[512]{0:T(512)S(1)} %get-tuple-element.12, s32[512]{0:T(512)S(1)} %iota.8), dimensions={0}, to_apply=%region_0.1 | sort | flops 4608 | bytes 8192 | tf_op jit(solution)/shard_map/jit(argsort)/sort | solution.py:17
  5.2 3.5 %gather_fusion = s32[512]{0:T(512)S(1)} fusion(s32[512]{0:T(512)S(1)} %get-tuple-element.13, s32[1024]{0:T(1024)S(1)} %pad_clamp_fusion.2), kind=kCustom, calls=%fused_computation | custom fusion | bytes 6144 | tf_op jit(solution)/shard_map/gather | solution.py:18
  8.7 0.1 all_to_all.9
  8.8 20.9 %all_to_all.14 = s32[128,1,4]{2,1,0:T(1,128)S(1)} all-to-all(s32[128,1,4]{2,1,0:T(1,128)S(1)} %bitcast.10), channel_id=1, replica_groups=mesh['grp'=8,'dom'=16] {'grp','dom'}, dimensions={0} | all-to-all | bytes 4096 | tf_op jit(solution)/shard_map/all_to_all | solution.py:19
  29.7 0.5 broadcast.57
  30.2 0.8 reduce.3
  31.0 0.1 reshape.58
  31.2 0.0 copy-done
  31.2 2.1 %gather_fusion.1 = bf16[512,1024]{1,0:T(8,128)(2,1)S(1)} fusion(bf16[512,1024]{1,0:T(8,128)(2,1)S(1)} %copy-done, s32[1024]{0:T(1024)S(1)} %pad_clamp_fusion.1), kind=kCustom, calls=%fused_computation.1 | custom fusion | bytes 2099200 | tf_op jit(solution)/shard_map/gather | solution.py:20
  33.2 1.2 reshape.59
  34.4 4.4 %all-to-all-start.1 = ((bf16[128,4,1024]{2,1,0:T(4,128)(2,1)}), bf16[128,4,1024]{2,1,0:T(4,128)(2,1)S(1)}, u32[]{:S(2)}, u32[]{:S(2)}) async-start(bf16[128,4,1024]{2,1,0:T(4,128)(2,1)} %reshape.59), calls=%async_computation.1 | async-start | bytes 2097152 | tf_op jit(solution)/shard_map/all_to_all | solution.py:21
  38.9 3.8 %sort.35 = (s32[512]{0:T(512)}, s32[512]{0:T(512)S(1)}) sort(s32[512]{0:T(512)S(1)} %get-tuple-element.6, s32[512]{0:T(512)S(1)} %iota.9), dimensions={0}, to_apply=%region_1.2 | sort | flops 4608 | bytes 8192 | tf_op jit(solution)/shard_map/jit(argsort)/sort | solution.py:23
  42.6 15.3 %all-to-all-done.1 = bf16[128,4,1024]{2,1,0:T(4,128)(2,1)S(1)} async-done(((bf16[128,4,1024]{2,1,0:T(4,128)(2,1)}), bf16[128,4,1024]{2,1,0:T(4,128)(2,1)S(1)}, u32[]{:S(2)}, u32[]{:S(2)}) %all-to-all-start.1) | async-done | bytes 1048608 | tf_op jit(solution)/shard_map/all_to_all | solution.py:21
  57.9 0.3 reshape.60
  58.2 2.8 %gather_fusion.2 = bf16[512,1024]{1,0:T(8,128)(2,1)} fusion(bf16[512,1024]{1,0:T(8,128)(2,1)S(1)} %reshape.60, s32[1024]{0:T(1024)S(1)} %pad_clamp_fusion), kind=kCustom, calls=%fused_computation.2 | custom fusion | bytes 2099200 | tf_op jit(solution)/shard_map/gather | solution.py:24
  60.9 61.1 %gather_group.1 = bf16[16,512,1024]{2,1,0:T(8,128)(2,1)} custom-call(bf16[512,1024]{1,0:T(8,128)(2,1)} %gather_fusion.2), custom_call_target="tpu_custom_call" | custom-call | tf_op jit(solution)/shard_map/gather_group/pallas_call | solution.py:146
  122.0 11.1 %local_pass.1 = (bf16[512,512]{1,0:T(8,128)(2,1)}, bf16[2,1024,256]{2,1,0:T(8,128)(2,1)}) custom-call(s32[4,16]{1,0:T(4,128)} %cols.1, s32[4]{0:T(128)} %count.1, bf16[64,128,1024]{2,1,0:T(8,128)(2,1)} %bitcast.6, bf16[4,16,128,128]{3,2,1,0:T(8,128)(2,1)} %vals.1, bf16[1024,512]{1,0:T(8,128)(2,1)} %weight.1, bf16[512,512]{1,0:T(8,128)(2,1)} %cot.1), custom_call_target="tpu_custom_call" | custom-call | tf_op jit(solution)/shard_map/local_pass/pallas_call | solution.py:207
  133.1 37.3 %sum_terms.1 = bf16[2,64,16,256]{3,2,1,0:T(8,128)(2,1)} custom-call(bf16[2,64,16,256]{3,2,1,0:T(8,128)(2,1)} %bitcast.9), custom_call_target="tpu_custom_call" | custom-call | tf_op jit(solution)/shard_map/sum_terms/pallas_call | solution.py:305
  170.4 1.5 fusion.1
  171.9 1.6 pad_maximum_fusion
  (8 shorter events, 0.0 us)
Async XLA Ops:
  0.6 30.5 %copy-start = (bf16[512,1024]{1,0:T(8,128)(2,1)S(1)}, bf16[512,1024]{1,0:T(8,128)(2,1)}, u32[]{:S(2)}) copy-start(bf16[512,1024]{1,0:T(8,128)(2,1)} %param.7) | copy-start | bytes 3145732
  34.4 23.5 %all-to-all-start.1 = ((bf16[128,4,1024]{2,1,0:T(4,128)(2,1)}), bf16[128,4,1024]{2,1,0:T(4,128)(2,1)S(1)}, u32[]{:S(2)}, u32[]{:S(2)}) async-start(bf16[128,4,1024]{2,1,0:T(4,128)(2,1)} %reshape.59), calls=%async_computation.1 | async-start | bytes 2097152 | tf_op jit(solution)/shard_map/all_to_all | solution.py:21

commit v5 on v4

--- a/solution.py
+++ b/solution.py
@@ -8,20 +8,92 @@
 AXES = ("grp", "dom")
 
 
+def order_kernel(order, asked, orders, keep_sem, out_sem, in_sem):
+    devices, _, rows = orders.shape
+    grp, dom = lax.axis_index("grp"), lax.axis_index("dom")
+    me = grp * 16 + dom
+    mesh_ids = pl.DeviceIdType.MESH
+
+    def ahead(offset):
+        x_hi, y = lax.rem(grp // 4 + offset // 64, 2), lax.rem(grp % 4 + (offset // 16) % 4, 4)
+        z, x_lo = lax.rem(dom // 4 + (offset // 4) % 4, 4), lax.rem((dom // 2) % 2 + (offset // 2) % 2, 2)
+        return {"grp": x_hi * 4 + y, "dom": z * 4 + x_lo * 2 + lax.rem(dom % 2 + offset % 2, 2)}
+
+    barrier = pltpu.get_barrier_semaphore()
+
+    @pl.loop(1, devices)
+    def _(offset):
+        pl.semaphore_signal(barrier, inc=1, device_id=ahead(offset), device_id_type=mesh_ids)
+
+    keep = pltpu.make_async_copy(order, orders.at[me], keep_sem)
+    keep.start()
+    pl.semaphore_wait(barrier, devices - 1)
+
+    @pl.loop(1, devices)
+    def _(offset):
+        pltpu.make_async_remote_copy(
+            src_ref=order, dst_ref=orders.at[me], send_sem=out_sem, recv_sem=in_sem,
+            device_id=ahead(offset), device_id_type=mesh_ids,
+        ).start()
+
+    keep.wait()
+    others = orders.at[pl.ds(0, devices - 1)]
+    every = pltpu.make_async_remote_copy(
+        src_ref=others, dst_ref=others, send_sem=out_sem, recv_sem=in_sem,
+        device_id=ahead(1), device_id_type=mesh_ids,
+    )
+    every.wait_recv()
+    row = orders[...].reshape(devices, rows) - me * rows
+    mine = jnp.logical_and(row >= 0, row < rows)
+    earlier = lax.broadcasted_iota(jnp.int32, (rows, rows), 0) <= lax.broadcasted_iota(jnp.int32, (rows, rows), 1)
+    rank = jnp.dot(
+        jnp.where(mine, 1.0, 0.0).astype(jnp.bfloat16),
+        jnp.where(earlier, 1.0, 0.0).astype(jnp.bfloat16),
+        preferred_element_type=jnp.float32,
+    )
+    rank = jnp.where(mine, rank, 0.0)
+    lane = lax.broadcasted_iota(jnp.int32, asked.shape, 1)
+    table = jnp.zeros(asked.shape, jnp.float32)
+    for number in range(rows // devices):
+        picked = jnp.where(rank == number + 1.0, row.astype(jnp.float32), 0.0)
+        table = jnp.where(lane == number, jnp.sum(picked, axis=1, keepdims=True), table)
+    asked[...] = table.astype(jnp.int32)
+    every.wait_send()
+
+
+def ask(node_order):
+    devices = lax.axis_size("grp") * lax.axis_size("dom")
+    rows = node_order.shape[0]
+    vmem = pl.BlockSpec(memory_space=pltpu.VMEM)
+    return pl.pallas_call(
+        order_kernel,
+        out_shape=jax.ShapeDtypeStruct((devices, 128), jnp.int32),
+        in_specs=[vmem],
+        out_specs=vmem,
+        scratch_shapes=[
+            pltpu.VMEM((devices, 1, rows), jnp.int32),
+            pltpu.SemaphoreType.DMA,
+            pltpu.SemaphoreType.DMA,
+            pltpu.SemaphoreType.DMA,
+        ],
+        compiler_params=pltpu.CompilerParams(collective_id=2, has_side_effects=True),
+        name="ask",
+    )(node_order.reshape(1, rows))
+
+
 def regroup(features, node_order):
     row_count, width_in = features.shape
     devices = lax.axis_size("grp") * lax.axis_size("dom")
     per_pair = row_count // devices
-    source_device = node_order // row_count
-    source_row = node_order % row_count
-    ordering = jnp.argsort(source_device, stable=True)
-    requests = source_row[ordering].reshape(devices, per_pair)
-    asked_rows = lax.all_to_all(requests, AXES, split_axis=0, concat_axis=0, tiled=True)
+    asked_rows = ask(node_order)[:, :per_pair]
     outgoing = features[asked_rows.reshape(-1)].reshape(devices, per_pair, width_in)
     arrived = lax.all_to_all(outgoing, AXES, split_axis=0, concat_axis=0, tiled=True)
     arrived = arrived.reshape(row_count, width_in)
-    inverse = jnp.argsort(ordering)
-    return arrived[inverse]
+    source = node_order // row_count
+    position = jnp.arange(row_count, dtype=jnp.int32)
+    before = jnp.logical_and(source[:, None] == source[None, :], position[None, :] < position[:, None])
+    slot = source * per_pair + jnp.sum(before.astype(jnp.int32), axis=1)
+    return arrived[slot]
 
 
 def piece_plan(rows):
@@ -290,9 +362,10 @@
         device_id=partner, device_id_type=mesh_ids,
     )
     give.start()
-    total[core] = whole[core]
     give.wait()
-    total[1 - core] = whole[1 - core]
+    columns = whole.shape[3]
+    for side in range(2):
+        total[:, :, side * columns:(side + 1) * columns] = whole[side]
     all_pieces(1).wait_send()
 
 
@@ -304,7 +377,7 @@
     vmem = pl.BlockSpec(memory_space=pltpu.VMEM)
     whole = pl.pallas_call(
         sum_kernel,
-        out_shape=jax.ShapeDtypeStruct(shape, term.dtype),
+        out_shape=jax.ShapeDtypeStruct((chips, share, 2 * columns), term.dtype),
         in_specs=[vmem],
         out_specs=vmem,
         scratch_shapes=[
@@ -320,8 +393,7 @@
         compiler_params=pltpu.CompilerParams(collective_id=1, has_side_effects=True),
         name="sum_terms",
     )(term.reshape(shape))
-    sides = whole.reshape(2, width_in, columns).astype(jnp.float32)
-    return jnp.concatenate([sides[0], sides[1]], axis=1)
+    return whole.reshape(width_in, 2 * columns).astype(jnp.float32)
 
 
 def shards(features, node_order, block_cols, block_count, block_vals, weight, cotangent):

time: 174 us -> 175 us (level)
  Pallas kernels: 109 us -> 139 us
  blocking collectives: 20.9 us -> 0 us
  other arithmetic: 10.8 us -> 3.13 us
  local copies, waits for them, and re-layouts: 12 us -> 7.27 us
  waiting for transfers between devices: 15.3 us -> 18.7 us
    pallas_call x1 -> x2, Pallas kernels: 37.3 us -> 65.7 us  [the longest x1 38.5 us: sum_terms(): pl.pallas_call(sum_kernel, out_shape=jax.ShapeDtypeStruct((chips, share,...]
    all_to_all x1 -> x0, blocking collectives: 20.9 us -> none  [regroup(): lax.all_to_all(requests, AXES, split_axis=0, concat_axis=0, tiled=True)]
    sort x2 -> x0, other arithmetic: 7.54 us -> none  [the longest x1 3.77 us: regroup(): ordering = jnp.argsort(source_device, stable=True)]
    gather x2 -> x1, local copies, waits for them, and re-layouts: 6.27 us -> 2.78 us  [regroup(): return arrived[slot]]
    all_to_all x1, waiting for transfers between devices: 15.3 us -> 18.7 us  [regroup(): lax.all_to_all(outgoing, AXES, split_axis=0, concat_axis=0, tiled=True)]
    convert_element_type x0 -> x1, other arithmetic: none -> 2.84 us  [sum_terms(): return whole.reshape(width_in, 2 * columns).astype(jnp.float32)]
  transfers between devices with their start and end apart: 1 -> 1, of which waited for: 1 -> 1; matrix products, arithmetic and copies ran while one was open for 2% -> 0% of each run, Pallas kernels for 0% -> 0%
where the time goes in v5:
time: 175 us; the launch traced here: 174 us
  Pallas kernels  139 us (79%)
  waiting for transfers between devices  18.7 us (11%)
  local copies, waits for them, and re-layouts  7.27 us (4%)
  starting transfers between devices  5.89 us (3%)
  other arithmetic  3.13 us (2%)
    pallas_call x1, Pallas kernels, gather_group(): pl.pallas_call(gather_kernel, out_shape=jax.ShapeDtypeStruct((group, rows...  61.1 us
    pallas_call x1, Pallas kernels, sum_terms(): pl.pallas_call(sum_kernel, out_shape=jax.ShapeDtypeStruct((chips, share,...  38.5 us
    pallas_call x1, Pallas kernels, ask(): pl.pallas_call(order_kernel, out_shape=jax.ShapeDtypeStruct((devices, 128...  27.3 us
    all_to_all x1, waiting for transfers between devices, regroup(): lax.all_to_all(outgoing, AXES, split_axis=0, concat_axis=0, tiled=True)  18.7 us
    pallas_call x1, Pallas kernels, local_pass(): pl.pallas_call(local_kernel, out_shape=(jax.ShapeDtypeStruct((rows, hidde...  11.8 us
    all_to_all x1, starting transfers between devices, regroup(): lax.all_to_all(outgoing, AXES, split_axis=0, concat_axis=0, tiled=True)  5.89 us
  transfers between devices with their start and end apart: 1, of which 1 were waited for; matrix products, arithmetic and copies ran while one was open for 0% of the time, Pallas kernels for 0%

profile of v5, /device:TPU:1, one launch (start us, length us, event | category | flops | bytes accessed | tf_op | source)
XLA Modules:
  0.0 174.3 jit_solution(4395273727932648199)
XLA Ops:
  0.6 0.0 copy-start
  0.6 27.3 %ask.1 = s32[128,128]{1,0:T(8,128)} custom-call(s32[1,512]{1,0:T(1,128)} %bitcast.11), custom_call_target="tpu_custom_call" | custom-call | tf_op jit(solution)/shard_map/ask/pallas_call | solution.py:68
  27.9 0.9 reshape.56
  28.9 0.0 copy-done
  28.9 2.1 %gather_fusion = bf16[512,1024]{1,0:T(8,128)(2,1)S(1)} fusion(bf16[512,1024]{1,0:T(8,128)(2,1)S(1)} %copy-done, s32[1024]{0:T(1024)S(1)} %pad_clamp_fusion.1), kind=kCustom, calls=%fused_computation | custom fusion | bytes 2099200 | tf_op jit(solution)/shard_map/gather | solution.py:89
  31.0 0.0 copy-start.1
  31.0 1.2 reshape.57
  32.2 5.9 %all-to-all-start = ((bf16[128,4,1024]{2,1,0:T(4,128)(2,1)}), bf16[128,4,1024]{2,1,0:T(4,128)(2,1)S(1)}, u32[]{:S(2)}, u32[]{:S(2)}) async-start(bf16[128,4,1024]{2,1,0:T(4,128)(2,1)} %reshape.57), calls=%async_computation | async-start | bytes 2097152 | tf_op jit(solution)/shard_map/all_to_all | solution.py:90
  38.1 0.0 copy-done.1
  38.1 0.2 convert_reduce_fusion
  38.4 18.7 %all-to-all-done = bf16[128,4,1024]{2,1,0:T(4,128)(2,1)S(1)} async-done(((bf16[128,4,1024]{2,1,0:T(4,128)(2,1)}), bf16[128,4,1024]{2,1,0:T(4,128)(2,1)S(1)}, u32[]{:S(2)}, u32[]{:S(2)}) %all-to-all-start) | async-done | bytes 1048608 | tf_op jit(solution)/shard_map/all_to_all | solution.py:90
  57.1 0.3 reshape.58
  57.4 2.8 %gather_fusion.1 = bf16[512,1024]{1,0:T(8,128)(2,1)} fusion(bf16[512,1024]{1,0:T(8,128)(2,1)S(1)} %reshape.58, s32[1024]{0:T(1024)S(1)} %pad_clamp_fusion), kind=kCustom, calls=%fused_computation.1 | custom fusion | bytes 2099200 | tf_op jit(solution)/shard_map/gather | solution.py:96
  60.2 61.1 %gather_group.1 = bf16[16,512,1024]{2,1,0:T(8,128)(2,1)} custom-call(bf16[512,1024]{1,0:T(8,128)(2,1)} %gather_fusion.1), custom_call_target="tpu_custom_call" | custom-call | tf_op jit(solution)/shard_map/gather_group/pallas_call | solution.py:218
  121.2 11.8 %local_pass.1 = (bf16[512,512]{1,0:T(8,128)(2,1)}, bf16[2,1024,256]{2,1,0:T(8,128)(2,1)}) custom-call(s32[4,16]{1,0:T(4,128)} %cols.1, s32[4]{0:T(128)} %count.1, bf16[64,128,1024]{2,1,0:T(8,128)(2,1)} %bitcast.8, bf16[4,16,128,128]{3,2,1,0:T(8,128)(2,1)} %vals.1, bf16[1024,512]{1,0:T(8,128)(2,1)} %weight.1, bf16[512,512]{1,0:T(8,128)(2,1)} %cot.1), custom_call_target="tpu_custom_call" | custom-call | tf_op jit(solution)/shard_map/local_pass/pallas_call | solution.py:279
  133.0 38.5 %sum_terms.1 = bf16[64,16,512]{2,1,0:T(8,128)(2,1)} custom-call(bf16[2,64,16,256]{3,2,1,0:T(8,128)(2,1)} %bitcast.9), custom_call_target="tpu_custom_call" | custom-call | tf_op jit(solution)/shard_map/sum_terms/pallas_call | solution.py:378
  171.5 2.8 %bitcast_convert_fusion = f32[1024,512]{1,0:T(8,128)} fusion(bf16[64,16,512]{2,1,0:T(8,128)(2,1)} %sum_terms.1), kind=kLoop, calls=%fused_computation.2 | loop fusion | flops 524288 | bytes 3145728 | tf_op jit(solution)/shard_map/convert_element_type | solution.py:396
  (5 shorter events, 0.0 us)
Async XLA Ops:
  0.6 28.3 %copy-start = (bf16[512,1024]{1,0:T(8,128)(2,1)S(1)}, bf16[512,1024]{1,0:T(8,128)(2,1)}, u32[]{:S(2)}) copy-start(bf16[512,1024]{1,0:T(8,128)(2,1)} %param.7) | copy-start | bytes 3145732
  31.0 7.1 %copy-start.1 = (s32[512]{0:T(512)S(1)}, s32[512]{0:T(512)}, u32[]{:S(2)}) copy-start(s32[512]{0:T(512)} %param.8) | copy-start | bytes 6148
  32.2 24.9 %all-to-all-start = ((bf16[128,4,1024]{2,1,0:T(4,128)(2,1)}), bf16[128,4,1024]{2,1,0:T(4,128)(2,1)S(1)}, u32[]{:S(2)}, u32[]{:S(2)}) async-start(bf16[128,4,1024]{2,1,0:T(4,128)(2,1)} %reshape.57), calls=%async_computation | async-start | bytes 2097152 | tf_op jit(solution)/shard_map/all_to_all | solution.py:90

commit v6 on v5

--- a/solution.py
+++ b/solution.py
@@ -8,42 +8,53 @@
 AXES = ("grp", "dom")
 
 
-def order_kernel(order, asked, orders, keep_sem, out_sem, in_sem):
-    devices, _, rows = orders.shape
+def order_kernel(order, asked, orders, keep_sem, out_sems, in_sems):
+    group, groups, _, rows = orders.shape
     grp, dom = lax.axis_index("grp"), lax.axis_index("dom")
-    me = grp * 16 + dom
     mesh_ids = pl.DeviceIdType.MESH
 
-    def ahead(offset):
-        x_hi, y = lax.rem(grp // 4 + offset // 64, 2), lax.rem(grp % 4 + (offset // 16) % 4, 4)
-        z, x_lo = lax.rem(dom // 4 + (offset // 4) % 4, 4), lax.rem((dom // 2) % 2 + (offset // 2) % 2, 2)
-        return {"grp": x_hi * 4 + y, "dom": z * 4 + x_lo * 2 + lax.rem(dom % 2 + offset % 2, 2)}
+    def across(offset):
+        x_hi, y = lax.rem(grp // 4 + offset // 4, 2), lax.rem(grp % 4 + offset % 4, 4)
+        return {"grp": x_hi * 4 + y, "dom": dom}
+
+    def along(offset):
+        z, x_lo = lax.rem(dom // 4 + offset // 4, 4), lax.rem((dom // 2) % 2 + (offset // 2) % 2, 2)
+        return {"grp": grp, "dom": z * 4 + x_lo * 2 + lax.rem(dom % 2 + offset % 2, 2)}
 
     barrier = pltpu.get_barrier_semaphore()
-
-    @pl.loop(1, devices)
-    def _(offset):
-        pl.semaphore_signal(barrier, inc=1, device_id=ahead(offset), device_id_type=mesh_ids)
-
-    keep = pltpu.make_async_copy(order, orders.at[me], keep_sem)
+    for offset in range(1, groups):
+        pl.semaphore_signal(barrier, inc=1, device_id=across(offset), device_id_type=mesh_ids)
+    for offset in range(1, group):
+        pl.semaphore_signal(barrier, inc=1, device_id=along(offset), device_id_type=mesh_ids)
+    keep = pltpu.make_async_copy(order, orders.at[dom, grp], keep_sem)
     keep.start()
-    pl.semaphore_wait(barrier, devices - 1)
-
-    @pl.loop(1, devices)
-    def _(offset):
+    pl.semaphore_wait(barrier, groups + group - 2)
+
+    for offset in range(1, groups):
         pltpu.make_async_remote_copy(
-            src_ref=order, dst_ref=orders.at[me], send_sem=out_sem, recv_sem=in_sem,
-            device_id=ahead(offset), device_id_type=mesh_ids,
+            src_ref=order, dst_ref=orders.at[dom, grp], send_sem=out_sems.at[0], recv_sem=in_sems.at[0],
+            device_id=across(offset), device_id_type=mesh_ids,
         ).start()
-
     keep.wait()
-    others = orders.at[pl.ds(0, devices - 1)]
+    some = orders.at[0, pl.ds(0, groups - 1)]
+    first = pltpu.make_async_remote_copy(
+        src_ref=some, dst_ref=some, send_sem=out_sems.at[0], recv_sem=in_sems.at[0],
+        device_id=across(1), device_id_type=mesh_ids,
+    )
+    first.wait_recv()
+    for offset in range(1, group):
+        pltpu.make_async_remote_copy(
+            src_ref=orders.at[dom], dst_ref=orders.at[dom], send_sem=out_sems.at[1], recv_sem=in_sems.at[1],
+            device_id=along(offset), device_id_type=mesh_ids,
+        ).start()
+    others = orders.at[pl.ds(0, group - 1)]
     every = pltpu.make_async_remote_copy(
-        src_ref=others, dst_ref=others, send_sem=out_sem, recv_sem=in_sem,
-        device_id=ahead(1), device_id_type=mesh_ids,
+        src_ref=others, dst_ref=others, send_sem=out_sems.at[1], recv_sem=in_sems.at[1],
+        device_id=along(1), device_id_type=mesh_ids,
     )
     every.wait_recv()
-    row = orders[...].reshape(devices, rows) - me * rows
+    row = jnp.concatenate([orders[:, number].reshape(group, rows) for number in range(groups)], axis=0)
+    row = row - (grp * group + dom) * rows
     mine = jnp.logical_and(row >= 0, row < rows)
     earlier = lax.broadcasted_iota(jnp.int32, (rows, rows), 0) <= lax.broadcasted_iota(jnp.int32, (rows, rows), 1)
     rank = jnp.dot(
@@ -54,10 +65,11 @@
     rank = jnp.where(mine, rank, 0.0)
     lane = lax.broadcasted_iota(jnp.int32, asked.shape, 1)
     table = jnp.zeros(asked.shape, jnp.float32)
-    for number in range(rows // devices):
+    for number in range(rows // (groups * group)):
         picked = jnp.where(rank == number + 1.0, row.astype(jnp.float32), 0.0)
         table = jnp.where(lane == number, jnp.sum(picked, axis=1, keepdims=True), table)
     asked[...] = table.astype(jnp.int32)
+    first.wait_send()
     every.wait_send()
 
 
@@ -71,10 +83,10 @@
         in_specs=[vmem],
         out_specs=vmem,
         scratch_shapes=[
-            pltpu.VMEM((devices, 1, rows), jnp.int32),
+            pltpu.VMEM((lax.axis_size("dom"), lax.axis_size("grp"), 1, rows), jnp.int32),
             pltpu.SemaphoreType.DMA,
-            pltpu.SemaphoreType.DMA,
-            pltpu.SemaphoreType.DMA,
+            pltpu.SemaphoreType.DMA((2,)),
+            pltpu.SemaphoreType.DMA((2,)),
         ],
         compiler_params=pltpu.CompilerParams(collective_id=2, has_side_effects=True),
         name="ask",
@@ -93,7 +105,7 @@
     position = jnp.arange(row_count, dtype=jnp.int32)
     before = jnp.logical_and(source[:, None] == source[None, :], position[None, :] < position[:, None])
     slot = source * per_pair + jnp.sum(before.astype(jnp.int32), axis=1)
-    return arrived[slot]
+    return arrived, slot
 
 
 def piece_plan(rows):
@@ -123,7 +135,7 @@
 LINKS = ("up", "down", "side")
 
 
-def gather_kernel(own, out, send_sems, recv_sems, pass_send, pass_recv, keep_sem):
+def gather_kernel(arrived, slot, out, own, send_sems, recv_sems, pass_send, pass_recv, keep_sem):
     rows = own.shape[0]
     me = lax.axis_index("dom")
     depth, column, core = me // 4, (me // 2) % 2, me % 2
@@ -139,6 +151,11 @@
     barrier = pltpu.get_barrier_semaphore()
     for target in (*targets.values(), partner):
         pl.semaphore_signal(barrier, inc=1, device_id={"dom": target}, device_id_type=pl.DeviceIdType.MESH)
+    taken = lax.broadcasted_iota(jnp.int32, (rows, rows), 0) == slot[...]
+    own[...] = lax.dot_general(
+        jnp.where(taken, 1.0, 0.0).astype(own.dtype), arrived[...],
+        (((0,), (0,)), ((), ())), preferred_element_type=jnp.float32,
+    ).astype(own.dtype)
     keep = pltpu.make_async_copy(own, out.at[me], keep_sem)
     keep.start()
     pl.semaphore_wait(barrier, 4)
@@ -212,15 +229,17 @@
     keep.wait()
 
 
-def gather_group(ordered):
-    rows, width_in = ordered.shape
+def gather_group(arrived, slot):
+    rows, width_in = arrived.shape
+    vmem = pl.BlockSpec(memory_space=pltpu.VMEM)
     group = lax.axis_size("dom")
     return pl.pallas_call(
         gather_kernel,
-        out_shape=jax.ShapeDtypeStruct((group, rows, width_in), ordered.dtype),
-        in_specs=[pl.BlockSpec(memory_space=pltpu.VMEM)],
+        out_shape=jax.ShapeDtypeStruct((group, rows, width_in), arrived.dtype),
+        in_specs=[vmem, vmem],
         out_specs=pl.BlockSpec(memory_space=pl.ANY),
         scratch_shapes=[
+            pltpu.VMEM((rows, width_in), arrived.dtype),
             pltpu.SemaphoreType.DMA((18,)),
             pltpu.SemaphoreType.DMA((18,)),
             pltpu.SemaphoreType.DMA((19,)),
@@ -229,7 +248,7 @@
         ],
         compiler_params=pltpu.CompilerParams(collective_id=0, has_side_effects=True),
         name="gather_group",
-    )(ordered)
+    )(arrived, slot.reshape(1, rows))
 
 
 def local_kernel(cols, count, panel, vals, weight, cot, hidden, term, chosen, acc, mixed, sems):
@@ -397,8 +416,8 @@
 
 
 def shards(features, node_order, block_cols, block_count, block_vals, weight, cotangent):
-    ordered = regroup(features, node_order)
-    everyone = gather_group(ordered)
+    arrived, slot = regroup(features, node_order)
+    everyone = gather_group(arrived, slot)
     hidden, term = local_pass(everyone, block_cols, block_count, block_vals, weight, cotangent)
     return (hidden, sum_terms(term))
 

time: 175 us -> 165 us (0.943)
  Pallas kernels: 139 us -> 130 us
  local copies, waits for them, and re-layouts: 7.27 us -> 5.32 us
    pallas_call x1, Pallas kernels: 27.3 us -> 19.2 us  [ask(): pl.pallas_call(order_kernel, out_shape=jax.ShapeDtypeStruct((devices, 128...]
    gather x1 -> x0, local copies, waits for them, and re-layouts: 2.78 us -> none  [regroup(): return arrived[slot]]
  transfers between devices with their start and end apart: 1 -> 1, of which waited for: 1 -> 1; matrix products, arithmetic and copies ran while one was open for 0% -> 1% of each run, Pallas kernels for 0% -> 0%
where the time goes in v6:
time: 165 us
  Pallas kernels  130 us (79%)
  waiting for transfers between devices  18.2 us (11%)
  starting transfers between devices  6.6 us (4%)
  local copies, waits for them, and re-layouts  5.32 us (3%)
  other arithmetic  3.7 us (2%)
    pallas_call x1, Pallas kernels, gather_group(): pl.pallas_call(gather_kernel, out_shape=jax.ShapeDtypeStruct((group, rows...  61.1 us
    pallas_call x1, Pallas kernels, sum_terms(): pl.pallas_call(sum_kernel, out_shape=jax.ShapeDtypeStruct((chips, share,...  39.9 us
    pallas_call x1, Pallas kernels, ask(): pl.pallas_call(order_kernel, out_shape=jax.ShapeDtypeStruct((devices, 128...  19.2 us
    all_to_all x1, waiting for transfers between devices, regroup(): lax.all_to_all(outgoing, AXES, split_axis=0, concat_axis=0, tiled=True)  18.2 us
    pallas_call x1, Pallas kernels, local_pass(): pl.pallas_call(local_kernel, out_shape=(jax.ShapeDtypeStruct((rows, hidde...  10.2 us
    all_to_all x1, starting transfers between devices, regroup(): lax.all_to_all(outgoing, AXES, split_axis=0, concat_axis=0, tiled=True)  6.6 us
  transfers between devices with their start and end apart: 1, of which 1 were waited for; matrix products, arithmetic and copies ran while one was open for 1% of the time, Pallas kernels for 0%

profile of v6, /device:TPU:1, one launch (start us, length us, event | category | flops | bytes accessed | tf_op | source)
XLA Modules:
  0.0 165.0 jit_solution(13067819484388172996)
XLA Ops:
  0.6 0.0 copy-start
  0.6 19.2 %ask.1 = s32[128,128]{1,0:T(8,128)} custom-call(s32[1,512]{1,0:T(1,128)} %bitcast.12), custom_call_target="tpu_custom_call" | custom-call | tf_op jit(solution)/shard_map/ask/pallas_call | solution.py:80
  19.9 0.9 reshape.59
  20.8 0.0 copy-done
  20.8 2.1 %gather_fusion = bf16[512,1024]{1,0:T(8,128)(2,1)S(1)} fusion(bf16[512,1024]{1,0:T(8,128)(2,1)S(1)} %copy-done, s32[1024]{0:T(1024)S(1)} %pad_clamp_fusion), kind=kCustom, calls=%fused_computation | custom fusion | bytes 2099200 | tf_op jit(solution)/shard_map/gather | solution.py:101
  22.9 0.0 copy-start.1
  22.9 1.2 reshape.60
  24.1 6.6 %all-to-all-start = ((bf16[128,4,1024]{2,1,0:T(4,128)(2,1)}), bf16[128,4,1024]{2,1,0:T(4,128)(2,1)S(1)}, u32[]{:S(2)}, u32[]{:S(2)}) async-start(bf16[128,4,1024]{2,1,0:T(4,128)(2,1)} %reshape.60), calls=%async_computation | async-start | bytes 2097152 | tf_op jit(solution)/shard_map/all_to_all | solution.py:102
  30.7 0.0 copy-done.1
  30.8 0.2 convert_reduce_fusion
  31.0 0.6 multiply_add_fusion
  31.6 18.2 %all-to-all-done = bf16[128,4,1024]{2,1,0:T(4,128)(2,1)S(1)} async-done(((bf16[128,4,1024]{2,1,0:T(4,128)(2,1)}), bf16[128,4,1024]{2,1,0:T(4,128)(2,1)S(1)}, u32[]{:S(2)}, u32[]{:S(2)}) %all-to-all-start) | async-done | bytes 1048608 | tf_op jit(solution)/shard_map/all_to_all | solution.py:102
  49.8 1.1 reshape.61.arrived
  50.9 61.1 %gather_group.1 = bf16[16,512,1024]{2,1,0:T(8,128)(2,1)} custom-call(bf16[512,1024]{1,0:T(8,128)(2,1)} %reshape.61.arrived, s32[1,512]{1,0:T(1,128)} %bitcast.13), custom_call_target="tpu_custom_call" | custom-call | tf_op jit(solution)/shard_map/gather_group/pallas_call | solution.py:236
  111.9 10.2 %local_pass.1 = (bf16[512,512]{1,0:T(8,128)(2,1)}, bf16[2,1024,256]{2,1,0:T(8,128)(2,1)}) custom-call(s32[4,16]{1,0:T(4,128)} %cols.1, s32[4]{0:T(128)} %count.1, bf16[64,128,1024]{2,1,0:T(8,128)(2,1)} %bitcast.9, bf16[4,16,128,128]{3,2,1,0:T(8,128)(2,1)} %vals.1, bf16[1024,512]{1,0:T(8,128)(2,1)} %weight.1, bf16[512,512]{1,0:T(8,128)(2,1)} %cot.1), custom_call_target="tpu_custom_call" | custom-call | tf_op jit(solution)/shard_map/local_pass/pallas_call | solution.py:298
  122.2 39.9 %sum_terms.1 = bf16[64,16,512]{2,1,0:T(8,128)(2,1)} custom-call(bf16[2,64,16,256]{3,2,1,0:T(8,128)(2,1)} %bitcast.10), custom_call_target="tpu_custom_call" | custom-call | tf_op jit(solution)/shard_map/sum_terms/pallas_call | solution.py:397
  162.1 2.8 %bitcast_convert_fusion = f32[1024,512]{1,0:T(8,128)} fusion(bf16[64,16,512]{2,1,0:T(8,128)(2,1)} %sum_terms.1), kind=kLoop, calls=%fused_computation.1 | loop fusion | flops 524288 | bytes 3145728 | tf_op jit(solution)/shard_map/convert_element_type | solution.py:415
  (3 shorter events, 0.0 us)
Async XLA Ops:
  0.6 20.2 %copy-start = (bf16[512,1024]{1,0:T(8,128)(2,1)S(1)}, bf16[512,1024]{1,0:T(8,128)(2,1)}, u32[]{:S(2)}) copy-start(bf16[512,1024]{1,0:T(8,128)(2,1)} %param.7) | copy-start | bytes 3145732
  22.9 7.8 %copy-start.1 = (s32[512]{0:T(512)S(1)}, s32[512]{0:T(512)}, u32[]{:S(2)}) copy-start(s32[512]{0:T(512)} %param.8) | copy-start | bytes 6148
  24.1 25.7 %all-to-all-start = ((bf16[128,4,1024]{2,1,0:T(4,128)(2,1)}), bf16[128,4,1024]{2,1,0:T(4,128)(2,1)S(1)}, u32[]{:S(2)}, u32[]{:S(2)}) async-start(bf16[128,4,1024]{2,1,0:T(4,128)(2,1)} %reshape.60), calls=%async_computation | async-start | bytes 2097152 | tf_op jit(solution)/shard_map/all_to_all | solution.py:102

commit v7 on v6

--- a/solution.py
+++ b/solution.py
@@ -251,41 +251,47 @@
     )(arrived, slot.reshape(1, rows))
 
 
-def local_kernel(cols, count, panel, vals, weight, cot, hidden, term, chosen, acc, mixed, sems):
+def local_kernel(cols, count, panel, vals, weight, cot, hidden, mixed, grad, chosen, acc, sems):
     tiles, blocks, size, _ = vals.shape
 
     def fetch(t, k):
         return pltpu.make_async_copy(panel.at[cols[t, k]], chosen.at[t, k], sems.at[t, k])
 
+    def pairs(t):
+        return (count[t] + 1) // 2
+
+    def product(t, pair):
+        k = 2 * pair
+        fetch(t, k).wait()
+        fetch(t, k + 1).wait()
+        second = vals[t, k + 1]
+        second = jnp.where(k + 1 < count[t], second, jnp.zeros_like(second))
+        left = jnp.concatenate([vals[t, k], second], axis=1)
+        right = chosen[t, pl.ds(k, 2)].reshape(2 * size, chosen.shape[3])
+        return jnp.dot(left, right, preferred_element_type=jnp.float32)
+
     for t in range(tiles):
-        @pl.loop(0, count[t])
+        @pl.loop(0, 2 * pairs(t))
         def _(k):
             fetch(t, k).start()
 
     for t in range(tiles):
-        live = count[t]
-        fetch(t, 0).wait()
-        acc[...] = jnp.dot(vals[t, 0], chosen[t, 0], preferred_element_type=jnp.float32)
-
-        @pl.loop(1, live)
-        def _(k):
-            fetch(t, k).wait()
-            acc[...] += jnp.dot(vals[t, k], chosen[t, k], preferred_element_type=jnp.float32)
+        acc[...] = product(t, 0)
+
+        @pl.loop(1, pairs(t))
+        def _(pair):
+            acc[...] += product(t, pair)
 
         mixed[pl.ds(t * size, size), :] = acc[...].astype(jnp.bfloat16)
 
-    rows = mixed[...]
-    aggregate = jnp.dot(rows, weight[...], preferred_element_type=jnp.float32)
+    aggregate = jnp.dot(mixed[...], weight[...], preferred_element_type=jnp.float32)
     sig = jax.nn.sigmoid(aggregate)
     hidden[...] = (aggregate * sig).astype(hidden.dtype)
     slope = sig * (1.0 + aggregate * (1.0 - sig))
-    grad_agg = (cot[...].astype(jnp.float32) * slope).astype(jnp.bfloat16)
-    products = lax.dot_general(
-        rows, grad_agg, (((0,), (0,)), ((), ())), preferred_element_type=jnp.float32
-    ).astype(term.dtype)
-    columns = term.shape[2]
+    grad_agg = (cot[...].astype(jnp.float32) * slope).astype(grad.dtype)
+    columns = grad.shape[2]
     for side in range(2):
-        term[side] = products[:, side * columns:(side + 1) * columns]
+        grad[side] = grad_agg[:, side * columns:(side + 1) * columns]
 
 
 def local_pass(everyone, block_cols, block_count, block_vals, weight, cotangent):
@@ -299,22 +305,22 @@
         local_kernel,
         out_shape=(
             jax.ShapeDtypeStruct((rows, hidden_units), jnp.bfloat16),
-            jax.ShapeDtypeStruct((2, width_in, hidden_units // 2), jnp.bfloat16),
+            jax.ShapeDtypeStruct((rows, width_in), jnp.bfloat16),
+            jax.ShapeDtypeStruct((2, rows, hidden_units // 2), jnp.bfloat16),
         ),
         in_specs=[smem, smem, pl.BlockSpec(memory_space=pl.ANY), vmem, vmem, vmem],
-        out_specs=(vmem, vmem),
+        out_specs=(vmem, vmem, vmem),
         scratch_shapes=[
             pltpu.VMEM((tiles, blocks, size, width_in), jnp.bfloat16),
             pltpu.VMEM((size, width_in), jnp.float32),
-            pltpu.VMEM((rows, width_in), jnp.bfloat16),
             pltpu.SemaphoreType.DMA((tiles, blocks)),
         ],
         name="local_pass",
     )(block_cols, block_count, panel, block_vals, weight, cotangent)
 
 
-def sum_kernel(term, total, paired, half, pieces, chunk, whole, pair_sems, out_sems, in_sems):
-    chips = term.shape[1]
+def sum_kernel(mixed, grad, total, term, paired, half, pieces, chunk, whole, pair_sems, out_sems, in_sems):
+    chips = half.shape[0]
     grp, dom = lax.axis_index("grp"), lax.axis_index("dom")
     core = dom % 2
     chip = grp * 8 + dom // 2
@@ -333,15 +339,22 @@
     def _(offset):
         pl.semaphore_signal(barrier, inc=1, device_id=ahead(offset), device_id_type=mesh_ids)
 
+    def own_term(side):
+        return lax.dot_general(
+            mixed[...], grad[side], (((0,), (0,)), ((), ())), preferred_element_type=jnp.float32
+        ).reshape(half.shape)
+
+    term[...] = own_term(1 - core).astype(term.dtype)
     pl.semaphore_wait(barrier, chips)
 
     swap = pltpu.make_async_remote_copy(
-        src_ref=term.at[1 - core], dst_ref=paired, send_sem=pair_sems.at[0], recv_sem=pair_sems.at[1],
+        src_ref=term, dst_ref=paired, send_sem=pair_sems.at[0], recv_sem=pair_sems.at[1],
         device_id=partner, device_id_type=mesh_ids,
     )
     swap.start()
+    kept = own_term(core)
     swap.wait()
-    half[...] = (term[core].astype(jnp.float32) + paired[...].astype(jnp.float32)).astype(half.dtype)
+    half[...] = (kept + paired[...].astype(jnp.float32)).astype(half.dtype)
 
     def place(offset):
         to = ahead(offset)
@@ -388,38 +401,39 @@
     all_pieces(1).wait_send()
 
 
-def sum_terms(term):
+def sum_terms(mixed, grad):
     chips = lax.axis_size("grp") * lax.axis_size("dom") // 2
-    _, width_in, columns = term.shape
+    width_in, columns = mixed.shape[1], grad.shape[2]
     share = width_in // chips
     shape = (2, chips, share, columns)
     vmem = pl.BlockSpec(memory_space=pltpu.VMEM)
     whole = pl.pallas_call(
         sum_kernel,
-        out_shape=jax.ShapeDtypeStruct((chips, share, 2 * columns), term.dtype),
-        in_specs=[vmem],
+        out_shape=jax.ShapeDtypeStruct((chips, share, 2 * columns), grad.dtype),
+        in_specs=[vmem, vmem],
         out_specs=vmem,
         scratch_shapes=[
-            pltpu.VMEM(shape[1:], term.dtype),
-            pltpu.VMEM(shape[1:], term.dtype),
-            pltpu.VMEM((chips - 1, share, columns), term.dtype),
-            pltpu.VMEM((share, columns), term.dtype),
-            pltpu.VMEM(shape, term.dtype),
+            pltpu.VMEM(shape[1:], grad.dtype),
+            pltpu.VMEM(shape[1:], grad.dtype),
+            pltpu.VMEM(shape[1:], grad.dtype),
+            pltpu.VMEM((chips - 1, share, columns), grad.dtype),
+            pltpu.VMEM((share, columns), grad.dtype),
+            pltpu.VMEM(shape, grad.dtype),
             pltpu.SemaphoreType.DMA((4,)),
             pltpu.SemaphoreType.DMA((2,)),
             pltpu.SemaphoreType.DMA((2,)),
         ],
         compiler_params=pltpu.CompilerParams(collective_id=1, has_side_effects=True),
         name="sum_terms",
-    )(term.reshape(shape))
+    )(mixed, grad)
     return whole.reshape(width_in, 2 * columns).astype(jnp.float32)
 
 
 def shards(features, node_order, block_cols, block_count, block_vals, weight, cotangent):
     arrived, slot = regroup(features, node_order)
     everyone = gather_group(arrived, slot)
-    hidden, term = local_pass(everyone, block_cols, block_count, block_vals, weight, cotangent)
-    return (hidden, sum_terms(term))
+    hidden, mixed, grad = local_pass(everyone, block_cols, block_count, block_vals, weight, cotangent)
+    return (hidden, sum_terms(mixed, grad))
 
 
 def solution(mesh):

time: 165 us -> 160 us (0.970)
  Pallas kernels: 130 us -> 125 us
    pallas_call x1, Pallas kernels: 39.9 us -> 34.6 us  [sum_terms(): pl.pallas_call(sum_kernel, out_shape=jax.ShapeDtypeStruct((chips, share,...]
where the time goes in v7:
time: 160 us; the launch traced here: 159 us
  Pallas kernels  125 us (78%)
  waiting for transfers between devices  18.2 us (11%)
  starting transfers between devices  6.6 us (4%)
  local copies, waits for them, and re-layouts  5.32 us (3%)
  other arithmetic  3.7 us (2%)
    pallas_call x1, Pallas kernels, gather_group(): pl.pallas_call(gather_kernel, out_shape=jax.ShapeDtypeStruct((group, rows...  61.1 us
    pallas_call x1, Pallas kernels, sum_terms(): pl.pallas_call(sum_kernel, out_shape=jax.ShapeDtypeStruct((chips, share,...  34.6 us
    pallas_call x1, Pallas kernels, ask(): pl.pallas_call(order_kernel, out_shape=jax.ShapeDtypeStruct((devices, 128...  19.2 us
    all_to_all x1, waiting for transfers between devices, regroup(): lax.all_to_all(outgoing, AXES, split_axis=0, concat_axis=0, tiled=True)  18.2 us
    pallas_call x1, Pallas kernels, local_pass(): pl.pallas_call(local_kernel, out_shape=(jax.ShapeDtypeStruct((rows, hidde...  9.97 us
    all_to_all x1, starting transfers between devices, regroup(): lax.all_to_all(outgoing, AXES, split_axis=0, concat_axis=0, tiled=True)  6.6 us
  transfers between devices with their start and end apart: 1, of which 1 were waited for; matrix products, arithmetic and copies ran while one was open for 1% of the time, Pallas kernels for 0%

profile of v7, /device:TPU:1, one launch (start us, length us, event | category | flops | bytes accessed | tf_op | source)
XLA Modules:
  0.0 159.4 jit_solution(15850728903780335078)
XLA Ops:
  0.6 0.0 copy-start
  0.6 19.2 %ask.1 = s32[128,128]{1,0:T(8,128)} custom-call(s32[1,512]{1,0:T(1,128)} %bitcast.10), custom_call_target="tpu_custom_call" | custom-call | tf_op jit(solution)/shard_map/ask/pallas_call | solution.py:80
  19.9 0.9 reshape.56
  20.8 0.0 copy-done
  20.8 2.1 %gather_fusion = bf16[512,1024]{1,0:T(8,128)(2,1)S(1)} fusion(bf16[512,1024]{1,0:T(8,128)(2,1)S(1)} %copy-done, s32[1024]{0:T(1024)S(1)} %pad_clamp_fusion), kind=kCustom, calls=%fused_computation | custom fusion | bytes 2099200 | tf_op jit(solution)/shard_map/gather | solution.py:101
  22.9 0.0 copy-start.1
  22.9 1.2 reshape.57
  24.1 6.6 %all-to-all-start = ((bf16[128,4,1024]{2,1,0:T(4,128)(2,1)}), bf16[128,4,1024]{2,1,0:T(4,128)(2,1)S(1)}, u32[]{:S(2)}, u32[]{:S(2)}) async-start(bf16[128,4,1024]{2,1,0:T(4,128)(2,1)} %reshape.57), calls=%async_computation | async-start | bytes 2097152 | tf_op jit(solution)/shard_map/all_to_all | solution.py:102
  30.7 0.0 copy-done.1
  30.8 0.2 convert_reduce_fusion
  31.0 0.6 multiply_add_fusion
  31.6 18.2 %all-to-all-done = bf16[128,4,1024]{2,1,0:T(4,128)(2,1)S(1)} async-done(((bf16[128,4,1024]{2,1,0:T(4,128)(2,1)}), bf16[128,4,1024]{2,1,0:T(4,128)(2,1)S(1)}, u32[]{:S(2)}, u32[]{:S(2)}) %all-to-all-start) | async-done | bytes 1048608 | tf_op jit(solution)/shard_map/all_to_all | solution.py:102
  49.8 1.1 reshape.58.arrived
  50.9 61.1 %gather_group.1 = bf16[16,512,1024]{2,1,0:T(8,128)(2,1)} custom-call(bf16[512,1024]{1,0:T(8,128)(2,1)} %reshape.58.arrived, s32[1,512]{1,0:T(1,128)} %bitcast.11), custom_call_target="tpu_custom_call" | custom-call | tf_op jit(solution)/shard_map/gather_group/pallas_call | solution.py:236
  111.9 10.0 %local_pass.1 = (bf16[512,512]{1,0:T(8,128)(2,1)}, bf16[512,1024]{1,0:T(8,128)(2,1)}, bf16[2,512,256]{2,1,0:T(8,128)(2,1)}) custom-call(s32[4,16]{1,0:T(4,128)} %cols.1, s32[4]{0:T(128)} %count.1, bf16[64,128,1024]{2,1,0:T(8,128)(2,1)} %bitcast.8, bf16[4,16,128,128]{3,2,1,0:T(8,128)(2,1)} %vals.1, bf16[1024,512]{1,0:T(8,128)(2,1)} %weight.1, ...), custom_call_target="tpu_custom_call" | custom-call | tf_op jit(solution)/shard_map/local_pass/pallas_call | solution.py:304
  121.9 34.6 %sum_terms.1 = bf16[64,16,512]{2,1,0:T(8,128)(2,1)} custom-call(bf16[512,1024]{1,0:T(8,128)(2,1)} %get-tuple-element.6.mixed, bf16[2,512,256]{2,1,0:T(8,128)(2,1)} %get-tuple-element.7.grad), custom_call_target="tpu_custom_call" | custom-call | tf_op jit(solution)/shard_map/sum_terms/pallas_call | solution.py:410
  156.6 2.8 %bitcast_convert_fusion = f32[1024,512]{1,0:T(8,128)} fusion(bf16[64,16,512]{2,1,0:T(8,128)(2,1)} %sum_terms.1), kind=kLoop, calls=%fused_computation.1 | loop fusion | flops 524288 | bytes 3145728 | tf_op jit(solution)/shard_map/convert_element_type | solution.py:429
  (3 shorter events, 0.0 us)
Async XLA Ops:
  0.6 20.2 %copy-start = (bf16[512,1024]{1,0:T(8,128)(2,1)S(1)}, bf16[512,1024]{1,0:T(8,128)(2,1)}, u32[]{:S(2)}) copy-start(bf16[512,1024]{1,0:T(8,128)(2,1)} %param.7) | copy-start | bytes 3145732
  22.9 7.8 %copy-start.1 = (s32[512]{0:T(512)S(1)}, s32[512]{0:T(512)}, u32[]{:S(2)}) copy-start(s32[512]{0:T(512)} %param.8) | copy-start | bytes 6148
  24.1 25.7 %all-to-all-start = ((bf16[128,4,1024]{2,1,0:T(4,128)(2,1)}), bf16[128,4,1024]{2,1,0:T(4,128)(2,1)S(1)}, u32[]{:S(2)}, u32[]{:S(2)}) async-start(bf16[128,4,1024]{2,1,0:T(4,128)(2,1)} %reshape.57), calls=%async_computation | async-start | bytes 2097152 | tf_op jit(solution)/shard_map/all_to_all | solution.py:102

commit v8 on v7

--- a/solution.py
+++ b/solution.py
@@ -319,7 +319,7 @@
     )(block_cols, block_count, panel, block_vals, weight, cotangent)
 
 
-def sum_kernel(mixed, grad, total, term, paired, half, pieces, chunk, whole, pair_sems, out_sems, in_sems):
+def sum_kernel(mixed, grad, total, term, kept, paired, half, pieces, chunk, whole, pair_sems, out_sems, in_sems):
     chips = half.shape[0]
     grp, dom = lax.axis_index("grp"), lax.axis_index("dom")
     core = dom % 2
@@ -347,58 +347,86 @@
     term[...] = own_term(1 - core).astype(term.dtype)
     pl.semaphore_wait(barrier, chips)
 
-    swap = pltpu.make_async_remote_copy(
-        src_ref=term, dst_ref=paired, send_sem=pair_sems.at[0], recv_sem=pair_sems.at[1],
-        device_id=partner, device_id_type=mesh_ids,
-    )
-    swap.start()
-    kept = own_term(core)
-    swap.wait()
-    half[...] = (kept + paired[...].astype(jnp.float32)).astype(half.dtype)
+    mid = chips // 2
+    near = (grp // 4) * mid
+    starts = (mid - near, near)
+    spans = tuple(pl.ds(start, mid) for start in starts)
+    offsets = ((mid, chips), (1, mid))
+
+    def swap(number):
+        return pltpu.make_async_remote_copy(
+            src_ref=term.at[spans[number]], dst_ref=paired.at[spans[number]],
+            send_sem=pair_sems.at[number], recv_sem=pair_sems.at[2 + number],
+            device_id=partner, device_id_type=mesh_ids,
+        )
+
+    swap(0).start()
+    swap(1).start()
+    kept[...] = own_term(core)
 
     def place(offset):
         to = ahead(offset)
         return to["grp"] * 8 + to["dom"] // 2
 
-    @pl.loop(1, chips)
-    def _(offset):
-        pltpu.make_async_remote_copy(
-            src_ref=half.at[place(offset)], dst_ref=pieces.at[offset - 1],
-            send_sem=out_sems.at[0], recv_sem=in_sems.at[0],
-            device_id=ahead(offset), device_id_type=mesh_ids,
-        ).start()
-
-    def all_pieces(number):
-        return pltpu.make_async_remote_copy(
-            src_ref=pieces, dst_ref=pieces, send_sem=out_sems.at[number], recv_sem=in_sems.at[number],
+    def arriving(number, stage):
+        low, high = offsets[number]
+        some = pieces.at[pl.ds(low - 1, high - low)]
+        return pltpu.make_async_remote_copy(
+            src_ref=some, dst_ref=some,
+            send_sem=out_sems.at[2 * stage + number], recv_sem=in_sems.at[2 * stage + number],
             device_id=partner, device_id_type=mesh_ids,
         )
 
-    all_pieces(0).wait_recv()
-    summed = half[chip].astype(jnp.float32) + jnp.sum(pieces[...].astype(jnp.float32), axis=0)
+    for number in range(2):
+        span = spans[number]
+        swap(number).wait_recv()
+        half[span] = (kept[span] + paired[span].astype(jnp.float32)).astype(half.dtype)
+
+        @pl.loop(*offsets[number])
+        def _(offset):
+            pltpu.make_async_remote_copy(
+                src_ref=half.at[place(offset)], dst_ref=pieces.at[offset - 1],
+                send_sem=out_sems.at[number], recv_sem=in_sems.at[number],
+                device_id=ahead(offset), device_id_type=mesh_ids,
+            ).start()
+
+    summed = half[chip].astype(jnp.float32)
+    for number in range(2):
+        low, high = offsets[number]
+        arriving(number, 0).wait_recv()
+        summed = summed + jnp.sum(pieces[pl.ds(low - 1, high - low)].astype(jnp.float32), axis=0)
     chunk[...] = summed.astype(chunk.dtype)
-    all_pieces(0).wait_send()
-
-    @pl.loop(1, chips)
-    def _(offset):
-        pltpu.make_async_remote_copy(
-            src_ref=chunk, dst_ref=whole.at[core, chip],
-            send_sem=out_sems.at[1], recv_sem=in_sems.at[1],
-            device_id=ahead(offset), device_id_type=mesh_ids,
-        ).start()
+
+    for number in range(2):
+        @pl.loop(*offsets[number])
+        def _(offset):
+            pltpu.make_async_remote_copy(
+                src_ref=chunk, dst_ref=whole.at[core, chip],
+                send_sem=out_sems.at[2 + number], recv_sem=in_sems.at[2 + number],
+                device_id=ahead(offset), device_id_type=mesh_ids,
+            ).start()
 
     whole[core, chip] = chunk[...]
-    all_pieces(1).wait_recv()
-    give = pltpu.make_async_remote_copy(
-        src_ref=whole.at[core], dst_ref=whole.at[core], send_sem=pair_sems.at[2], recv_sem=pair_sems.at[3],
-        device_id=partner, device_id_type=mesh_ids,
-    )
-    give.start()
-    give.wait()
+
+    def give(number):
+        part = whole.at[core, spans[number]]
+        return pltpu.make_async_remote_copy(
+            src_ref=part, dst_ref=part,
+            send_sem=pair_sems.at[4 + number], recv_sem=pair_sems.at[6 + number],
+            device_id=partner, device_id_type=mesh_ids,
+        )
+
+    for number in range(2):
+        arriving(number, 1).wait_recv()
+        give(number).start()
+    for number in range(2):
+        swap(number).wait_send()
+        give(number).wait()
+        for stage in range(2):
+            arriving(number, stage).wait_send()
     columns = whole.shape[3]
     for side in range(2):
         total[:, :, side * columns:(side + 1) * columns] = whole[side]
-    all_pieces(1).wait_send()
 
 
 def sum_terms(mixed, grad):
@@ -414,14 +442,15 @@
         out_specs=vmem,
         scratch_shapes=[
             pltpu.VMEM(shape[1:], grad.dtype),
+            pltpu.VMEM(shape[1:], jnp.float32),
             pltpu.VMEM(shape[1:], grad.dtype),
             pltpu.VMEM(shape[1:], grad.dtype),
             pltpu.VMEM((chips - 1, share, columns), grad.dtype),
             pltpu.VMEM((share, columns), grad.dtype),
             pltpu.VMEM(shape, grad.dtype),
+            pltpu.SemaphoreType.DMA((8,)),
             pltpu.SemaphoreType.DMA((4,)),
-            pltpu.SemaphoreType.DMA((2,)),
-            pltpu.SemaphoreType.DMA((2,)),
+            pltpu.SemaphoreType.DMA((4,)),
         ],
         compiler_params=pltpu.CompilerParams(collective_id=1, has_side_effects=True),
         name="sum_terms",

time: 160 us -> 159 us (level)
    pallas_call x1, Pallas kernels: 9.97 us -> 7.65 us  [local_pass(): pl.pallas_call(local_kernel, out_shape=(jax.ShapeDtypeStruct((rows, hidde...]
where the time goes in v8:
time: 159 us
  Pallas kernels  124 us (78%)
  waiting for transfers between devices  18.2 us (11%)
  starting transfers between devices  6.6 us (4%)
  local copies, waits for them, and re-layouts  5.32 us (3%)
  other arithmetic  3.7 us (2%)
    pallas_call x1, Pallas kernels, gather_group(): pl.pallas_call(gather_kernel, out_shape=jax.ShapeDtypeStruct((group, rows...  61.1 us
    pallas_call x1, Pallas kernels, sum_terms(): pl.pallas_call(sum_kernel, out_shape=jax.ShapeDtypeStruct((chips, share,...  36.1 us
    pallas_call x1, Pallas kernels, ask(): pl.pallas_call(order_kernel, out_shape=jax.ShapeDtypeStruct((devices, 128...  19.2 us
    all_to_all x1, waiting for transfers between devices, regroup(): lax.all_to_all(outgoing, AXES, split_axis=0, concat_axis=0, tiled=True)  18.2 us
    pallas_call x1, Pallas kernels, local_pass(): pl.pallas_call(local_kernel, out_shape=(jax.ShapeDtypeStruct((rows, hidde...  7.65 us
    all_to_all x1, starting transfers between devices, regroup(): lax.all_to_all(outgoing, AXES, split_axis=0, concat_axis=0, tiled=True)  6.6 us
  transfers between devices with their start and end apart: 1, of which 1 were waited for; matrix products, arithmetic and copies ran while one was open for 1% of the time, Pallas kernels for 0%

profile of v8, /device:TPU:1, one launch (start us, length us, event | category | flops | bytes accessed | tf_op | source)
XLA Modules:
  0.0 158.6 jit_solution(2645241454839929375)
XLA Ops:
  0.6 0.0 copy-start
  0.6 19.2 %ask.1 = s32[128,128]{1,0:T(8,128)} custom-call(s32[1,512]{1,0:T(1,128)} %bitcast.10), custom_call_target="tpu_custom_call" | custom-call | tf_op jit(solution)/shard_map/ask/pallas_call | solution.py:80
  19.9 0.9 reshape.56
  20.8 0.0 copy-done
  20.8 2.1 %gather_fusion = bf16[512,1024]{1,0:T(8,128)(2,1)S(1)} fusion(bf16[512,1024]{1,0:T(8,128)(2,1)S(1)} %copy-done, s32[1024]{0:T(1024)S(1)} %pad_clamp_fusion), kind=kCustom, calls=%fused_computation | custom fusion | bytes 2099200 | tf_op jit(solution)/shard_map/gather | solution.py:101
  22.9 0.0 copy-start.1
  22.9 1.2 reshape.57
  24.1 6.6 %all-to-all-start = ((bf16[128,4,1024]{2,1,0:T(4,128)(2,1)}), bf16[128,4,1024]{2,1,0:T(4,128)(2,1)S(1)}, u32[]{:S(2)}, u32[]{:S(2)}) async-start(bf16[128,4,1024]{2,1,0:T(4,128)(2,1)} %reshape.57), calls=%async_computation | async-start | bytes 2097152 | tf_op jit(solution)/shard_map/all_to_all | solution.py:102
  30.7 0.0 copy-done.1
  30.8 0.2 convert_reduce_fusion
  31.0 0.6 multiply_add_fusion
  31.6 18.2 %all-to-all-done = bf16[128,4,1024]{2,1,0:T(4,128)(2,1)S(1)} async-done(((bf16[128,4,1024]{2,1,0:T(4,128)(2,1)}), bf16[128,4,1024]{2,1,0:T(4,128)(2,1)S(1)}, u32[]{:S(2)}, u32[]{:S(2)}) %all-to-all-start) | async-done | bytes 1048608 | tf_op jit(solution)/shard_map/all_to_all | solution.py:102
  49.8 1.1 reshape.58.arrived
  50.9 61.1 %gather_group.1 = bf16[16,512,1024]{2,1,0:T(8,128)(2,1)} custom-call(bf16[512,1024]{1,0:T(8,128)(2,1)} %reshape.58.arrived, s32[1,512]{1,0:T(1,128)} %bitcast.11), custom_call_target="tpu_custom_call" | custom-call | tf_op jit(solution)/shard_map/gather_group/pallas_call | solution.py:236
  111.9 7.7 %local_pass.1 = (bf16[512,512]{1,0:T(8,128)(2,1)}, bf16[512,1024]{1,0:T(8,128)(2,1)}, bf16[2,512,256]{2,1,0:T(8,128)(2,1)}) custom-call(s32[4,16]{1,0:T(4,128)} %cols.1, s32[4]{0:T(128)} %count.1, bf16[64,128,1024]{2,1,0:T(8,128)(2,1)} %bitcast.8, bf16[4,16,128,128]{3,2,1,0:T(8,128)(2,1)} %vals.1, bf16[1024,512]{1,0:T(8,128)(2,1)} %weight.1, ...), custom_call_target="tpu_custom_call" | custom-call | tf_op jit(solution)/shard_map/local_pass/pallas_call | solution.py:304
  119.6 36.1 %sum_terms.1 = bf16[64,16,512]{2,1,0:T(8,128)(2,1)} custom-call(bf16[512,1024]{1,0:T(8,128)(2,1)} %get-tuple-element.6.mixed, bf16[2,512,256]{2,1,0:T(8,128)(2,1)} %get-tuple-element.7.grad), custom_call_target="tpu_custom_call" | custom-call | tf_op jit(solution)/shard_map/sum_terms/pallas_call | solution.py:438
  155.8 2.8 %bitcast_convert_fusion = f32[1024,512]{1,0:T(8,128)} fusion(bf16[64,16,512]{2,1,0:T(8,128)(2,1)} %sum_terms.1), kind=kLoop, calls=%fused_computation.1 | loop fusion | flops 524288 | bytes 3145728 | tf_op jit(solution)/shard_map/convert_element_type | solution.py:458
  (3 shorter events, 0.0 us)
Async XLA Ops:
  0.6 20.2 %copy-start = (bf16[512,1024]{1,0:T(8,128)(2,1)S(1)}, bf16[512,1024]{1,0:T(8,128)(2,1)}, u32[]{:S(2)}) copy-start(bf16[512,1024]{1,0:T(8,128)(2,1)} %param.7) | copy-start | bytes 3145732
  22.9 7.8 %copy-start.1 = (s32[512]{0:T(512)S(1)}, s32[512]{0:T(512)}, u32[]{:S(2)}) copy-start(s32[512]{0:T(512)} %param.8) | copy-start | bytes 6148
  24.1 25.7 %all-to-all-start = ((bf16[128,4,1024]{2,1,0:T(4,128)(2,1)}), bf16[128,4,1024]{2,1,0:T(4,128)(2,1)S(1)}, u32[]{:S(2)}, u32[]{:S(2)}) async-start(bf16[128,4,1024]{2,1,0:T(4,128)(2,1)} %reshape.57), calls=%async_computation | async-start | bytes 2097152 | tf_op jit(solution)/shard_map/all_to_all | solution.py:102

commit v9 on v8

--- a/solution.py
+++ b/solution.py
@@ -257,30 +257,32 @@
     def fetch(t, k):
         return pltpu.make_async_copy(panel.at[cols[t, k]], chosen.at[t, k], sems.at[t, k])
 
-    def pairs(t):
-        return (count[t] + 1) // 2
-
-    def product(t, pair):
-        k = 2 * pair
-        fetch(t, k).wait()
-        fetch(t, k + 1).wait()
-        second = vals[t, k + 1]
-        second = jnp.where(k + 1 < count[t], second, jnp.zeros_like(second))
-        left = jnp.concatenate([vals[t, k], second], axis=1)
-        right = chosen[t, pl.ds(k, 2)].reshape(2 * size, chosen.shape[3])
-        return jnp.dot(left, right, preferred_element_type=jnp.float32)
+    depth = 4
+
+    def bundles(t):
+        return (count[t] + depth - 1) // depth
+
+    def product(t, bundle):
+        first = depth * bundle
+        parts = []
+        for extra in range(depth):
+            fetch(t, first + extra).wait()
+            part = vals[t, first + extra]
+            parts.append(jnp.where(first + extra < count[t], part, jnp.zeros_like(part)))
+        right = chosen[t, pl.ds(first, depth)].reshape(depth * size, chosen.shape[3])
+        return jnp.dot(jnp.concatenate(parts, axis=1), right, preferred_element_type=jnp.float32)
 
     for t in range(tiles):
-        @pl.loop(0, 2 * pairs(t))
+        @pl.loop(0, depth * bundles(t))
         def _(k):
             fetch(t, k).start()
 
     for t in range(tiles):
         acc[...] = product(t, 0)
 
-        @pl.loop(1, pairs(t))
-        def _(pair):
-            acc[...] += product(t, pair)
+        @pl.loop(1, bundles(t))
+        def _(bundle):
+            acc[...] += product(t, bundle)
 
         mixed[pl.ds(t * size, size), :] = acc[...].astype(jnp.bfloat16)
 

time: 159 us -> 158 us (level)
    pallas_call x1, Pallas kernels: 36.1 us -> 33.7 us  [sum_terms(): pl.pallas_call(sum_kernel, out_shape=jax.ShapeDtypeStruct((chips, share,...]
where the time goes in v9:
time: 158 us
  Pallas kernels  123 us (78%)
  waiting for transfers between devices  18.2 us (12%)
  starting transfers between devices  6.6 us (4%)
  local copies, waits for them, and re-layouts  5.32 us (3%)
  other arithmetic  3.7 us (2%)
    pallas_call x1, Pallas kernels, gather_group(): pl.pallas_call(gather_kernel, out_shape=jax.ShapeDtypeStruct((group, rows...  61.1 us
    pallas_call x1, Pallas kernels, sum_terms(): pl.pallas_call(sum_kernel, out_shape=jax.ShapeDtypeStruct((chips, share,...  33.7 us
    pallas_call x1, Pallas kernels, ask(): pl.pallas_call(order_kernel, out_shape=jax.ShapeDtypeStruct((devices, 128...  19.2 us
    all_to_all x1, waiting for transfers between devices, regroup(): lax.all_to_all(outgoing, AXES, split_axis=0, concat_axis=0, tiled=True)  18.2 us
    pallas_call x1, Pallas kernels, local_pass(): pl.pallas_call(local_kernel, out_shape=(jax.ShapeDtypeStruct((rows, hidde...  9.24 us
    all_to_all x1, starting transfers between devices, regroup(): lax.all_to_all(outgoing, AXES, split_axis=0, concat_axis=0, tiled=True)  6.6 us
  transfers between devices with their start and end apart: 1, of which 1 were waited for; matrix products, arithmetic and copies ran while one was open for 1% of the time, Pallas kernels for 0%

profile of v9, /device:TPU:1, one launch (start us, length us, event | category | flops | bytes accessed | tf_op | source)
XLA Modules:
  0.0 157.7 jit_solution(680707653088098666)
XLA Ops:
  0.6 0.0 copy-start
  0.6 19.2 %ask.1 = s32[128,128]{1,0:T(8,128)} custom-call(s32[1,512]{1,0:T(1,128)} %bitcast.10), custom_call_target="tpu_custom_call" | custom-call | tf_op jit(solution)/shard_map/ask/pallas_call | solution.py:80
  19.9 0.9 reshape.56
  20.8 0.0 copy-done
  20.8 2.1 %gather_fusion = bf16[512,1024]{1,0:T(8,128)(2,1)S(1)} fusion(bf16[512,1024]{1,0:T(8,128)(2,1)S(1)} %copy-done, s32[1024]{0:T(1024)S(1)} %pad_clamp_fusion), kind=kCustom, calls=%fused_computation | custom fusion | bytes 2099200 | tf_op jit(solution)/shard_map/gather | solution.py:101
  22.9 0.0 copy-start.1
  22.9 1.2 reshape.57
  24.1 6.6 %all-to-all-start = ((bf16[128,4,1024]{2,1,0:T(4,128)(2,1)}), bf16[128,4,1024]{2,1,0:T(4,128)(2,1)S(1)}, u32[]{:S(2)}, u32[]{:S(2)}) async-start(bf16[128,4,1024]{2,1,0:T(4,128)(2,1)} %reshape.57), calls=%async_computation | async-start | bytes 2097152 | tf_op jit(solution)/shard_map/all_to_all | solution.py:102
  30.7 0.0 copy-done.1
  30.8 0.2 convert_reduce_fusion
  31.0 0.6 multiply_add_fusion
  31.6 18.2 %all-to-all-done = bf16[128,4,1024]{2,1,0:T(4,128)(2,1)S(1)} async-done(((bf16[128,4,1024]{2,1,0:T(4,128)(2,1)}), bf16[128,4,1024]{2,1,0:T(4,128)(2,1)S(1)}, u32[]{:S(2)}, u32[]{:S(2)}) %all-to-all-start) | async-done | bytes 1048608 | tf_op jit(solution)/shard_map/all_to_all | solution.py:102
  49.8 1.1 reshape.58.arrived
  50.9 61.1 %gather_group.1 = bf16[16,512,1024]{2,1,0:T(8,128)(2,1)} custom-call(bf16[512,1024]{1,0:T(8,128)(2,1)} %reshape.58.arrived, s32[1,512]{1,0:T(1,128)} %bitcast.11), custom_call_target="tpu_custom_call" | custom-call | tf_op jit(solution)/shard_map/gather_group/pallas_call | solution.py:236
  111.9 9.2 %local_pass.1 = (bf16[512,512]{1,0:T(8,128)(2,1)}, bf16[512,1024]{1,0:T(8,128)(2,1)}, bf16[2,512,256]{2,1,0:T(8,128)(2,1)}) custom-call(s32[4,16]{1,0:T(4,128)} %cols.1, s32[4]{0:T(128)} %count.1, bf16[64,128,1024]{2,1,0:T(8,128)(2,1)} %bitcast.8, bf16[4,16,128,128]{3,2,1,0:T(8,128)(2,1)} %vals.1, bf16[1024,512]{1,0:T(8,128)(2,1)} %weight.1, ...), custom_call_target="tpu_custom_call" | custom-call | tf_op jit(solution)/shard_map/local_pass/pallas_call | solution.py:306
  121.2 33.7 %sum_terms.1 = bf16[64,16,512]{2,1,0:T(8,128)(2,1)} custom-call(bf16[512,1024]{1,0:T(8,128)(2,1)} %get-tuple-element.6.mixed, bf16[2,512,256]{2,1,0:T(8,128)(2,1)} %get-tuple-element.7.grad), custom_call_target="tpu_custom_call" | custom-call | tf_op jit(solution)/shard_map/sum_terms/pallas_call | solution.py:440
  154.9 2.8 %bitcast_convert_fusion = f32[1024,512]{1,0:T(8,128)} fusion(bf16[64,16,512]{2,1,0:T(8,128)(2,1)} %sum_terms.1), kind=kLoop, calls=%fused_computation.1 | loop fusion | flops 524288 | bytes 3145728 | tf_op jit(solution)/shard_map/convert_element_type | solution.py:460
  (3 shorter events, 0.0 us)
Async XLA Ops:
  0.6 20.2 %copy-start = (bf16[512,1024]{1,0:T(8,128)(2,1)S(1)}, bf16[512,1024]{1,0:T(8,128)(2,1)}, u32[]{:S(2)}) copy-start(bf16[512,1024]{1,0:T(8,128)(2,1)} %param.7) | copy-start | bytes 3145732
  22.9 7.8 %copy-start.1 = (s32[512]{0:T(512)S(1)}, s32[512]{0:T(512)}, u32[]{:S(2)}) copy-start(s32[512]{0:T(512)} %param.8) | copy-start | bytes 6148
  24.1 25.7 %all-to-all-start = ((bf16[128,4,1024]{2,1,0:T(4,128)(2,1)}), bf16[128,4,1024]{2,1,0:T(4,128)(2,1)S(1)}, u32[]{:S(2)}, u32[]{:S(2)}) async-start(bf16[128,4,1024]{2,1,0:T(4,128)(2,1)} %reshape.57), calls=%async_computation | async-start | bytes 2097152 | tf_op jit(solution)/shard_map/all_to_all | solution.py:102
